TPU v7x, 32 devices: a whole 2x2x4 slice. The times are simulated.
32 devices in a mesh: grp: 2 (over y), ex: 4 (over z), proj: 4 (over x, core).
Axes of the slice: x: 2, y: 2, z: 4, core: 2. Of those that a mesh axis runs over, the one named last changes fastest.
Arguments:
- inputs: bfloat16 [32, 144, 5120], P(('grp', 'ex'), None, 'proj'), parts along dimension 0, may hold values from -6 to 6
- cotangents: bfloat16 [32, 144, 5120], P(('grp', 'ex'), None, 'proj'), parts along dimension 0, may hold values from -6 to 6
- lengths: int32 [32], P(('grp', 'ex')), parts along dimension 0, may hold values from 1 to 144, 1152 in all
- adapter_down_matrix: bfloat16 [128, 5120], P(None, 'proj'), may hold values from -0.078125 to 0.078125
- adapter_up_matrix: bfloat16 [5120, 128], P('proj'), may hold values from -0.078125 to 0.078125
- width_side_sketch: bfloat16 [5120, 512], P('proj'), may hold values from -0.078125 to 0.078125
- rank_side_sketch: bfloat16 [2, 128, 8], replicated, may hold values from -0.5 to 0.5
- heldout_gradient_rows: bfloat16 [256, 8192], P(('grp', 'ex'), 'proj'), parts along dimension 0, may hold values from -20 to 20
Outputs:
- train_proj: bfloat16 [32, 8192], P(('grp', 'ex'), 'proj'), parts along dimension 0
- scores: float32 [32, 128], P(('grp', 'ex'), 'proj'), parts along dimension 0
There are 2 independent parts, one for each index of `grp`. A program takes and returns all parts, laid end to end along the dimension named above; an argument that names none is the same for every part. Nothing has to cross between parts.
Inputs may be any that keep to these rules, and one draw needn't show every extreme that they name: The lengths of each part along grp sum to 1152.
All inputs are finite; a program needn't handle non-finite values. No bound on the sum of `lengths` on one device may be relied on, other than what follows from the above.
Results may differ from a plain program's by a relative error of at most 0.01.
Values may be sent and summed in bfloat16 or wider, within the bound.
A program may use at most 64 MiB of HBM per device.

v0:
```python
import functools
import math

import jax
import jax.numpy as jnp
from jax import lax
from jax.experimental import pallas as pl
from jax.experimental.pallas import tpu as pltpu
from jax.sharding import PartitionSpec as P

epsilon = 1e-06
MESH = pl.DeviceIdType.MESH
F32 = jnp.float32
BF16 = jnp.bfloat16
NT = (((1,), (1,)), ((), ()))


def dot(a, b, dims=(((1,), (0,)), ((), ()))):
    return lax.dot_general(a, b, dims, preferred_element_type=F32)


def kernel(
    sizes,
    len_ref, x_ref, c_ref, a_ref, b_ref, w_ref, r_ref, v_ref,
    tp_ref, sc_ref,
    xb, cb, ab, bb, wb, rows, left, gath,
    right_own, right_in, t_own, t_in, shuf, flat, sums, msg, msg_in,
    load_sem, rs_sem, rr_sem, ts_sem, tr_sem, ms_sem, mr_sem,
    gs_sem, gr_sem, own_sem,
):
    n_ex, n_proj, ex_dev, seq, pdim = sizes
    grp, me_ex, me = lax.axis_index("grp"), lax.axis_index("ex"), lax.axis_index("proj")
    k2 = r_ref.shape[1]
    pd = 2 * k2
    k1 = wb.shape[1]
    kc = k1 // n_proj
    reps = 128 // pd
    blocks = kc * pd // 128

    loads = []
    for i, (src, dst) in enumerate(
        ((a_ref, ab), (x_ref, xb), (b_ref, bb), (c_ref, cb), (w_ref, wb))
    ):
        copy = pltpu.make_async_copy(src, dst, load_sem.at[i])
        copy.start()
        loads.append(copy)
    own = pltpu.make_async_copy(v_ref, gath.at[me_ex], own_sem)
    own.start()

    def peer(k):
        return lax.rem(me + k, n_proj)

    barrier = pltpu.get_barrier_semaphore()
    for k in range(1, n_proj):
        pl.semaphore_signal(barrier, inc=1, device_id=(grp, me_ex, peer(k)), device_id_type=MESH)

    @pl.when(me_ex > 0)
    def _():
        pl.semaphore_signal(barrier, inc=1, device_id=(grp, me_ex - 1, me), device_id_type=MESH)

    @pl.when(me_ex < n_ex - 1)
    def _():
        pl.semaphore_signal(barrier, inc=1, device_id=(grp, me_ex + 1, me), device_id_type=MESH)

    sides = jnp.minimum(me_ex, 1) + jnp.minimum(n_ex - 1 - me_ex, 1)
    pl.semaphore_wait(barrier, n_proj - 1 + sides)

    chunks = gs_sem.shape[2]
    v_rows = gath.shape[1]
    part_rows = v_rows // chunks

    def hop(way, s, c, src=None):
        if way == 0:
            at, to = jnp.maximum(me_ex - s, 0), jnp.minimum(me_ex + 1, n_ex - 1)
        else:
            at, to = jnp.minimum(me_ex + s, n_ex - 1), jnp.maximum(me_ex - 1, 0)
        span = pl.ds(c * part_rows, part_rows)
        here = gath.at[at, span]
        return pltpu.make_async_remote_copy(
            src_ref=here if src is None else src.at[span],
            dst_ref=here,
            send_sem=gs_sem.at[way, s, c],
            recv_sem=gr_sem.at[way, s, c],
            device_id=(grp, to, me),
            device_id_type=MESH,
        )

    def sends(way, s):
        if way == 0:
            return (me_ex - s >= 0) & (me_ex < n_ex - 1)
        return (me_ex + s <= n_ex - 1) & (me_ex > 0)

    def receives(way, s):
        return (me_ex - 1 - s >= 0) if way == 0 else (me_ex + 1 + s <= n_ex - 1)

    def send_own():
        for way in range(2):
            @pl.when(sends(way, 0))
            def _():
                for c in range(chunks):
                    hop(way, 0, c, v_ref).start()

    def squares(at, first, count):
        held = gath[at, pl.ds(first, count)].astype(F32)
        held = held * held
        acc = held[:, :128]
        for c in range(1, gath.shape[2] // 128):
            acc = acc + held[:, c * 128:(c + 1) * 128]
        sums[pl.ds(pl.multiple_of(at * v_rows + first, part_rows), count), :] = acc

    def relay(s, c, forward=True):
        for way in range(2):
            @pl.when(receives(way, s))
            def _():
                hop(way, s, c).wait_recv()

            if forward:
                @pl.when(sends(way, s + 1))
                def _():
                    hop(way, s + 1, c).start()

            @pl.when(receives(way, s))
            def _():
                squares(me_ex - 1 - s if way == 0 else me_ex + 1 + s, c * part_rows, part_rows)

    def end_step(s):
        for way in range(2):
            @pl.when(sends(way, s))
            def _():
                for c in range(chunks):
                    hop(way, s, c).wait_send()

    send_own()

    def swap(k, src, dst, s_sem, r_sem):
        return pltpu.make_async_remote_copy(
            src_ref=src, dst_ref=dst.at[k - 1], send_sem=s_sem.at[k - 1], recv_sem=r_sem.at[k - 1],
            device_id=(grp, me_ex, peer(k)), device_id_type=MESH,
        )

    loads[0].wait()
    m_in = dot(r_ref[0], ab[...]).astype(BF16)
    loads[1].wait()
    part_in = dot(m_in, xb[...], NT)
    loads[2].wait()
    m_out = dot(r_ref[1], bb[...], NT).astype(BF16)
    loads[3].wait()
    part_out = dot(m_out, cb[...], NT)
    part = jnp.concatenate([part_in, part_out], axis=0)
    right_own[...] = part.astype(BF16)
    copies = [swap(k, right_own, right_in, rs_sem, rr_sem) for k in range(1, n_proj)]
    for copy in copies:
        copy.start()

    queue = [(t, c) for t in range(n_ex - 2) for c in range(chunks)] if n_ex <= 4 else []

    def poll():
        if queue:
            relay(*queue.pop(0))

    loads[4].wait()
    half = k1 // 2
    own.wait()
    left[0, :, :half] = dot(cb[...], wb[:, :half]).astype(BF16)
    squares(me_ex, 0, v_rows)
    poll()
    left[0, :, half:] = dot(cb[...], wb[:, half:]).astype(BF16)
    left[1, :, :half] = dot(xb[...], wb[:, :half]).astype(BF16)
    poll()
    left[1, :, half:] = dot(xb[...], wb[:, half:]).astype(BF16)

    for copy in copies:
        copy.wait()
    total = part
    for k in range(n_proj - 1):
        total = total + right_in[k].astype(F32)
    total = total.astype(BF16)

    position = lax.broadcasted_iota(jnp.int32, (k2, seq), 1)
    for e in range(ex_dev):
        live = position < len_ref[e]
        for p in range(2):
            piece = total[p * k2:(p + 1) * k2, e * seq:(e + 1) * seq].astype(F32)
            piece = jnp.where(live, piece, 0.0).astype(BF16)
            rows[e * pd + p * k2:e * pd + (p + 1) * k2, :] = dot(piece, left[p, e * seq:(e + 1) * seq, :])
    for j in range(n_proj):
        t_own[j] = rows[:, j * kc:(j + 1) * kc].astype(BF16)
    copies = [swap(k, t_own.at[peer(k)], t_in, ts_sem, tr_sem) for k in range(1, n_proj)]
    for copy in copies:
        copy.start()

    while queue:
        poll()

    mine = me * kc
    total_t = rows[:, pl.ds(pl.multiple_of(mine, 128), kc)]
    for copy in copies:
        copy.wait()
    for k in range(n_proj - 1):
        total_t = total_t + t_in[k].astype(F32)

    l_at = lax.broadcasted_iota(jnp.int32, (128, kc), 0)
    k_at = lax.broadcasted_iota(jnp.int32, (128, kc), 1)
    keep = (k_at % reps) == (l_at // pd)
    for e in range(ex_dev):
        one = total_t[e * pd:(e + 1) * pd, :] / len_ref[e].astype(F32)
        one = one.astype(BF16).astype(F32)
        tiled = jnp.concatenate([one] * reps, axis=0)
        shuf[e * 128:(e + 1) * 128, :] = jnp.where(keep, tiled, 0.0).astype(BF16)
    b_at = lax.broadcasted_iota(jnp.int32, (blocks, kc), 0)
    s_at = lax.broadcasted_iota(jnp.int32, (blocks, kc), 1)
    pick = jnp.where((s_at // reps) == b_at, 1.0, 0.0).astype(BF16)
    spread = dot(pick, shuf[...], NT)
    ep = flat.shape[0]
    flat[...] = jnp.zeros_like(flat)
    for b in range(blocks):
        for e in range(ex_dev):
            flat[e:e + 1, b * 128:(b + 1) * 128] = spread[b:b + 1, e * 128:(e + 1) * 128]
    train = flat[...]
    train_bf = train.astype(BF16)
    tp_ref[...] = train
    train_sq = jnp.sum(train * train, axis=1, keepdims=True)

    if n_ex > 4:
        @pl.loop(0, n_ex - 2)
        def _(t):
            for c in range(chunks):
                relay(t, c)

    for c in range(chunks):
        relay(n_ex - 2, c, False)
    nv = n_ex * v_rows
    per = 128 // v_rows
    cs = nv // n_proj
    ones = jnp.ones((8, 128), F32)
    dots = jnp.concatenate(
        [dot(train_bf, gath[i * per:(i + 1) * per].reshape(128, gath.shape[2]), NT) for i in range(nv // 128)],
        axis=1,
    )
    val_sq = lax.dot_general(
        ones, sums[...], NT, precision=lax.Precision.HIGHEST, preferred_element_type=F32
    )
    for j in range(n_proj):
        msg[j, :ep] = dots[:, j * cs:(j + 1) * cs]
        msg[j, ep:ep + 8] = val_sq[:, j * cs:(j + 1) * cs]
        msg[j, ep + 8:] = jnp.broadcast_to(train_sq, (ep, cs))
    copies = [swap(k, msg.at[peer(k)], msg_in, ms_sem, mr_sem) for k in range(1, n_proj)]
    for copy in copies:
        copy.start()
    for s in range(n_ex - 1):
        end_step(s)
    final = msg[me]
    for copy in copies:
        copy.wait()
    for k in range(n_proj - 1):
        final = final + msg_in[k]
    sc_ref[...] = final


def near_kernel(
    sizes,
    len_ref, x_ref, c_ref, a_ref, b_ref, w_ref, r_ref, v_ref,
    tp_ref, sc_ref,
    xb, cb, ab, bb, wb, rows, left, vals,
    right_own, right_in, t_own, t_in, t_send, t_recv, shuf, shuf_all, flat_all, f_send, f_recv,
    load_sem, rs_sem, rr_sem, ts_sem, tr_sem, us_sem, ur_sem, fs_sem, fr_sem, gs_sem, gr_sem, own_sem,
):
    n_ex, n_proj, ex_dev, seq, pdim = sizes
    grp, me_ex, me = lax.axis_index("grp"), lax.axis_index("ex"), lax.axis_index("proj")
    k2 = r_ref.shape[1]
    pd = 2 * k2
    kc = wb.shape[1] // n_proj
    reps = 128 // pd
    sub = kc // n_ex
    width = sub * pd
    v_rows = vals.shape[1]
    nv = n_ex * v_rows
    cs = nv // n_proj

    def peer(k):
        return lax.rem(me + k, n_proj)

    def peer_ex(k):
        return lax.rem(me_ex + k, n_ex)

    others = [(a, b) for a in reversed(range(n_ex)) for b in range(n_proj) if (a, b) != (0, 0)]
    barrier = pltpu.get_barrier_semaphore()
    for a, b in others:
        pl.semaphore_signal(
            barrier, inc=1, device_id=(grp, peer_ex(a), peer(b)), device_id_type=MESH
        )
    loads = []
    for i, (src, dst) in enumerate(
        ((a_ref, ab), (x_ref, xb), (b_ref, bb), (c_ref, cb), (w_ref, wb))
    ):
        copy = pltpu.make_async_copy(src, dst, load_sem.at[i])
        copy.start()
        loads.append(copy)

    def columns(at):
        return v_ref.at[:, pl.ds(pl.multiple_of(at * width, 128), width)]

    own = pltpu.make_async_copy(columns(me_ex), vals.at[me_ex], own_sem)
    own.start()

    def swap(k, src, dst, s_sem, r_sem):
        return pltpu.make_async_remote_copy(
            src_ref=src, dst_ref=dst.at[k - 1], send_sem=s_sem.at[k - 1], recv_sem=r_sem.at[k - 1],
            device_id=(grp, me_ex, peer(k)), device_id_type=MESH,
        )

    def spread_out(src, dst, s_sem, r_sem):
        started = []
        for n, (a, b) in enumerate(others):
            started.append(pltpu.make_async_remote_copy(
                src_ref=src.at[peer_ex(a), peer(b)], dst_ref=dst.at[me_ex, me],
                send_sem=s_sem.at[n], recv_sem=r_sem.at[n],
                device_id=(grp, peer_ex(a), peer(b)), device_id_type=MESH,
            ))
            started[-1].start()
        return started

    loads[0].wait()
    m_in = dot(r_ref[0], ab[...]).astype(BF16)
    loads[1].wait()
    part_in = dot(m_in, xb[...], NT)
    loads[2].wait()
    m_out = dot(r_ref[1], bb[...], NT).astype(BF16)
    loads[3].wait()
    part_out = dot(m_out, cb[...], NT)
    part = jnp.concatenate([part_in, part_out], axis=0)
    right_own[...] = part.astype(BF16)

    pl.semaphore_wait(barrier, len(others))
    copies = [swap(k, right_own, right_in, rs_sem, rr_sem) for k in range(1, n_proj)]
    for copy in copies:
        copy.start()
    moves = []
    for a in reversed(range(1, n_ex)):
        moves.append(pltpu.make_async_remote_copy(
            src_ref=columns(peer_ex(a)), dst_ref=vals.at[me_ex],
            send_sem=gs_sem.at[a - 1], recv_sem=gr_sem.at[a - 1],
            device_id=(grp, peer_ex(a), me), device_id_type=MESH,
        ))
        moves[-1].start()

    loads[4].wait()
    left[0] = dot(cb[...], wb[...]).astype(BF16)
    left[1] = dot(xb[...], wb[...]).astype(BF16)

    for copy in copies:
        copy.wait()
    total = part
    for k in range(n_proj - 1):
        total = total + right_in[k].astype(F32)
    total = total.astype(BF16)

    position = lax.broadcasted_iota(jnp.int32, (k2, seq), 1)
    for e in range(ex_dev):
        count = len_ref[e]
        live = position < count
        for p in range(2):
            piece = total[p * k2:(p + 1) * k2, e * seq:(e + 1) * seq].astype(F32)
            piece = jnp.where(live, piece, 0.0).astype(BF16)
            rows[e * pd + p * k2:e * pd + (p + 1) * k2, :] = (
                dot(piece, left[p, e * seq:(e + 1) * seq, :]) / count.astype(F32)
            )
    group = lax.broadcasted_iota(jnp.int32, (pd, kc), 1) // sub
    for q in range(n_proj):
        tiles = [rows[e * pd:(e + 1) * pd, q * kc:(q + 1) * kc] for e in range(ex_dev)]
        for j in range(n_ex):
            tile = jnp.zeros((pd, kc), F32)
            for e in range(ex_dev):
                shift = (e - j) * sub % kc
                turned = pltpu.roll(tiles[e], shift, 1) if shift else tiles[e]
                tile = jnp.where(group == e, turned, tile)
            t_send[j, q] = tile.astype(BF16)
    spreads = spread_out(t_send, t_recv, us_sem, ur_sem)
    for j in range(n_proj):
        t_own[j] = rows[:, j * kc:(j + 1) * kc].astype(BF16)
    copies = [swap(k, t_own.at[peer(k)], t_in, ts_sem, tr_sem) for k in range(1, n_proj)]
    for copy in copies:
        copy.start()
    t_recv[me_ex, me] = t_send[me_ex, me]

    own.wait()
    for move in moves:
        move.wait()
    held = vals[...].reshape(nv, width)
    wide = held.astype(F32)
    wide = wide * wide
    acc = wide[:, :128]
    for c in range(1, width // 128):
        acc = acc + wide[:, c * 128:(c + 1) * 128]
    val_sq = lax.dot_general(
        jnp.ones((8, 128), F32), acc, NT,
        precision=lax.Precision.HIGHEST, preferred_element_type=F32,
    )[:1]

    l_at = lax.broadcasted_iota(jnp.int32, (128, kc), 0)
    k_at = lax.broadcasted_iota(jnp.int32, (128, kc), 1)
    keep = (k_at % reps) == (l_at // pd)
    picks = kc // reps
    b_at = lax.broadcasted_iota(jnp.int32, (picks, kc), 0)
    s_at = lax.broadcasted_iota(jnp.int32, (picks, kc), 1)
    pick = jnp.where((s_at // reps) == b_at, 1.0, 0.0).astype(BF16)

    def fan(one):
        one = one.astype(BF16).astype(F32)
        tiled = jnp.concatenate([one] * reps, axis=0)
        return jnp.where(keep, tiled, 0.0).astype(BF16)

    for copy in spreads:
        copy.wait()
    for i in range(n_ex):
        one = t_recv[i, 0].astype(F32)
        for p in range(1, n_proj):
            one = one + t_recv[i, p].astype(F32)
        shuf_all[i * 128:(i + 1) * 128, :] = fan(one)
    spread = dot(pick, shuf_all[...], NT)
    runs = width // 128
    for i in range(n_ex):
        for e in range(ex_dev):
            for b in range(runs):
                flat_all[i * ex_dev + e:i * ex_dev + e + 1, b * 128:(b + 1) * 128] = (
                    spread[e * runs + b:e * runs + b + 1, i * 128:(i + 1) * 128]
                )
    train = flat_all[...]
    train_sq = jnp.sum(train * train, axis=1, keepdims=True)
    dots = dot(train.astype(BF16), held, NT)
    every = n_ex * ex_dev
    for q in range(n_proj):
        packed = jnp.concatenate([
            dots[:, q * cs:(q + 1) * cs],
            jnp.broadcast_to(val_sq[:, q * cs:(q + 1) * cs], (every, cs)),
            jnp.broadcast_to(train_sq, (every, 128 - 2 * cs)),
        ], axis=1)
        for i in range(n_ex):
            f_send[i, q] = packed[i * ex_dev:(i + 1) * ex_dev]
    spreads = spread_out(f_send, f_recv, fs_sem, fr_sem)
    f_recv[me_ex, me] = f_send[me_ex, me]

    mine = rows[:, pl.ds(pl.multiple_of(me * kc, 128), kc)]
    for copy in copies:
        copy.wait()
    for k in range(n_proj - 1):
        mine = mine + t_in[k].astype(F32)
    for e in range(ex_dev):
        shuf[e * 128:(e + 1) * 128, :] = fan(mine[e * pd:(e + 1) * pd, :])
    spread = dot(pick, shuf[...], NT)
    for b in range(picks):
        for e in range(ex_dev):
            tp_ref[e:e + 1, b * 128:(b + 1) * 128] = spread[b:b + 1, e * 128:(e + 1) * 128]

    for copy in spreads:
        copy.wait()
    final = jnp.zeros(f_recv.shape[2:], F32)
    for i in range(n_ex):
        for p in range(n_proj):
            final = final + f_recv[i, p]
    sc_ref[...] = final


def near_finish(pdim, train_ref, sums_ref, tp_ref, sc_ref):
    ex_dev, cs = sc_ref.shape
    tp_ref[...] = train_ref[:ex_dev, :].astype(BF16)
    final = sums_ref[...]
    sc_ref[...] = (
        math.sqrt(pdim)
        * final[:, :cs]
        * lax.rsqrt(final[:, 2 * cs:3 * cs] + epsilon)
        * lax.rsqrt(final[:, cs:2 * cs] + epsilon)
    )


def finish(pdim, train_ref, sums_ref, tp_ref, sc_ref):
    ex_dev = tp_ref.shape[0]
    ep = train_ref.shape[0]
    tp_ref[...] = train_ref[:ex_dev, :].astype(BF16)
    final = sums_ref[...]
    scores = (
        math.sqrt(pdim)
        * final[:ep]
        * lax.rsqrt(final[ep + 8:] + epsilon)
        * lax.rsqrt(final[ep:ep + 1] + epsilon)
    )
    sc_ref[...] = scores[:ex_dev]


def shards(
    mesh, inputs, cotangents, lengths, adapter_down_matrix, adapter_up_matrix,
    width_side_sketch, rank_side_sketch, heldout_gradient_rows,
):
    n_ex, n_proj = mesh.shape["ex"], mesh.shape["proj"]
    ex_dev, seq, cols = inputs.shape
    tokens = ex_dev * seq
    rank = adapter_down_matrix.shape[0]
    k1 = width_side_sketch.shape[1]
    k2 = rank_side_sketch.shape[2]
    pd = 2 * k2
    kc = k1 // n_proj
    v_rows, v_cols = heldout_gradient_rows.shape
    nv = v_rows * n_ex
    cs = nv // n_proj
    ep = -(-ex_dev // 8) * 8
    pdim = pd * k1
    any_space = pl.BlockSpec(memory_space=pltpu.HBM)
    vmem = pl.BlockSpec(memory_space=pltpu.VMEM)
    dma = pltpu.SemaphoreType.DMA
    peers = n_proj - 1
    sub = kc // n_ex
    near = (
        kc == 128 and sub * n_ex == kc and sub * ex_dev == 128 and sub * pd % 128 == 0
        and nv % 128 == 0 and 3 * cs <= 128
    )
    head = [
        pltpu.VMEM((tokens, cols), BF16),
        pltpu.VMEM((tokens, cols), BF16),
        pltpu.VMEM((rank, cols), BF16),
        pltpu.VMEM((cols, rank), BF16),
        pltpu.VMEM((cols, k1), BF16),
        pltpu.VMEM((ex_dev * pd, k1), F32),
        pltpu.VMEM((2, tokens, k1), BF16),
    ]
    if near:
        rest = n_ex * n_proj - 1
        body, end = near_kernel, near_finish
        sums_shape = (ex_dev, 128)
        scratch = head + [
            pltpu.VMEM((n_ex, v_rows, sub * pd), BF16),
            pltpu.VMEM((pd, tokens), BF16),
            pltpu.VMEM((peers, pd, tokens), BF16),
            pltpu.VMEM((n_proj, ex_dev * pd, kc), BF16),
            pltpu.VMEM((peers, ex_dev * pd, kc), BF16),
            pltpu.VMEM((n_ex, n_proj, pd, kc), BF16),
            pltpu.VMEM((n_ex, n_proj, pd, kc), BF16),
            pltpu.VMEM((ex_dev * 128, kc), BF16),
            pltpu.VMEM((n_ex * 128, kc), BF16),
            pltpu.VMEM((n_ex * ex_dev, sub * pd), F32),
            pltpu.VMEM((n_ex, n_proj, ex_dev, 128), F32),
            pltpu.VMEM((n_ex, n_proj, ex_dev, 128), F32),
            dma((5,)),
            dma((peers,)), dma((peers,)),
            dma((peers,)), dma((peers,)),
            dma((rest,)), dma((rest,)),
            dma((rest,)), dma((rest,)),
            dma((n_ex - 1,)), dma((n_ex - 1,)),
            dma,
        ]
    else:
        chunks = 2 if v_rows % 32 == 0 else 1
        body, end = kernel, finish
        sums_shape = (2 * ep + 8, cs)
        scratch = head + [
            pltpu.VMEM((n_ex, v_rows, v_cols), BF16),
            pltpu.VMEM((pd, tokens), BF16),
            pltpu.VMEM((peers, pd, tokens), BF16),
            pltpu.VMEM((n_proj, ex_dev * pd, kc), BF16),
            pltpu.VMEM((peers, ex_dev * pd, kc), BF16),
            pltpu.VMEM((ex_dev * 128, kc), BF16),
            pltpu.VMEM((ep, v_cols), F32),
            pltpu.VMEM((nv, 128), F32),
            pltpu.VMEM((n_proj, 2 * ep + 8, cs), F32),
            pltpu.VMEM((peers, 2 * ep + 8, cs), F32),
            dma((5,)),
            dma((peers,)), dma((peers,)),
            dma((peers,)), dma((peers,)),
            dma((peers,)), dma((peers,)),
            dma((2, n_ex - 1, chunks)), dma((2, n_ex - 1, chunks)),
            dma,
        ]
    train, final = pl.pallas_call(
        functools.partial(body, (n_ex, n_proj, ex_dev, seq, pdim)),
        out_shape=(
            pltpu.VMEM((ep, v_cols), F32),
            pltpu.VMEM(sums_shape, F32),
        ),
        in_specs=[pl.BlockSpec(memory_space=pltpu.SMEM)] + [any_space] * 5 + [vmem, any_space],
        out_specs=(vmem, vmem),
        scratch_shapes=scratch,
        compiler_params=pltpu.CompilerParams(
            collective_id=0, has_side_effects=True, vmem_limit_bytes=62 * 1024 * 1024
        ),
        name="project",
    )(
        lengths, inputs.reshape(tokens, cols), cotangents.reshape(tokens, cols),
        adapter_down_matrix, adapter_up_matrix, width_side_sketch,
        rank_side_sketch.swapaxes(1, 2), heldout_gradient_rows,
    )
    return pl.pallas_call(
        functools.partial(end, pdim),
        out_shape=(
            jax.ShapeDtypeStruct((ex_dev, v_cols), BF16),
            jax.ShapeDtypeStruct((ex_dev, cs), F32),
        ),
        in_specs=[vmem, vmem],
        out_specs=(vmem, vmem),
        compiler_params=pltpu.CompilerParams(vmem_limit_bytes=8 * 1024 * 1024),
        name="finish",
    )(train, final)


def solution(mesh):
    in_specs = (
        P(("grp", "ex"), None, "proj"),
        P(("grp", "ex"), None, "proj"),
        P(("grp", "ex")),
        P(None, "proj"),
        P("proj", None),
        P("proj", None),
        P(),
        P(("grp", "ex"), "proj"),
    )
    out_specs = (P(("grp", "ex"), "proj"), P(("grp", "ex"), "proj"))
    return jax.shard_map(
        functools.partial(shards, mesh), mesh=mesh, in_specs=in_specs, out_specs=out_specs, check_vma=False
    )
```

profile of v0, /device:TPU:0, one launch (start us, length us, event | category | flops | bytes accessed | tf_op | source)
XLA Modules:
  0.0 20.3 jit_solution(989101269780418459)
XLA Ops:
  0.6 19.0 %project.1 = (f32[8,2048]{1,0:T(8,128)S(1)}, f32[4,128]{1,0:T(4,128)S(1)}) custom-call(s32[4]{0:T(128)} %len_ref.1, bf16[576,1280]{1,0:T(8,128)(2,1)} %bitcast.3, bf16[576,1280]{1,0:T(8,128)(2,1)} %bitcast.4, bf16[128,1280]{1,0:T(8,128)(2,1)} %a_ref.1, bf16[1280,128]{1,0:T(8,128)(2,1)} %b_ref.1, bf16[1280,512]{1,0:T(8,128)(2,1)} %w_ref.1, ...), custom_call_target="tpu_custom_call" | custom-call | tf_op jit(solution)/shard_map/project/pallas_call | solution.py:572
  19.6 0.7 %finish.1 = (bf16[4,2048]{1,0:T(4,128)(2,1)}, f32[4,32]{1,0:T(4,128)}) custom-call(f32[8,2048]{1,0:T(8,128)S(1)} %get-tuple-element.4.train_ref, f32[4,128]{1,0:T(4,128)S(1)} %get-tuple-element.5.sums_ref), custom_call_target="tpu_custom_call" | custom-call | tf_op jit(solution)/shard_map/finish/pallas_call | solution.py:590
where the time goes:
time: 20.5 us; the launch traced here: 20.3 us
  Pallas kernels  19.7 us (96%)
  between operations  0.64 us (3%)
    pallas_call x1, Pallas kernels, shards(): pl.pallas_call(functools.partial(body, (n_ex, n_proj, ex_dev, seq, pdim))...  19 us
    pallas_call x1, Pallas kernels, shards(): pl.pallas_call(functools.partial(end, pdim), out_shape=(jax.ShapeDtypeStr...  0.66 us

commit v1 on v0

--- a/solution.py
+++ b/solution.py
@@ -257,38 +257,35 @@
     sc_ref[...] = final
 
 
-def near_kernel(
+def paired_kernel(
     sizes,
     len_ref, x_ref, c_ref, a_ref, b_ref, w_ref, r_ref, v_ref,
     tp_ref, sc_ref,
-    xb, cb, ab, bb, wb, rows, left, vals,
-    right_own, right_in, t_own, t_in, t_send, t_recv, shuf, shuf_all, flat_all, f_send, f_recv,
-    load_sem, rs_sem, rr_sem, ts_sem, tr_sem, us_sem, ur_sem, fs_sem, fr_sem, gs_sem, gr_sem, own_sem,
+    xb, cb, ab, bb, wb, held, rows, right_own, right_in, t_send, t_in, shuf, flat, f_send, f_recv,
+    load_sem, rs_sem, rr_sem, ts_sem, tr_sem, hs_sem, hr_sem, fs_sem, fr_sem, own_sem, ready,
 ):
     n_ex, n_proj, ex_dev, seq, pdim = sizes
     grp, me_ex, me = lax.axis_index("grp"), lax.axis_index("ex"), lax.axis_index("proj")
+    side, core = me // 2, lax.rem(me, 2)
+    home, slot = me_ex // 2, lax.rem(me_ex, 2)
+    sides = n_proj // 2
     k2 = r_ref.shape[1]
     pd = 2 * k2
     kc = wb.shape[1] // n_proj
     reps = 128 // pd
-    sub = kc // n_ex
-    width = sub * pd
-    v_rows = vals.shape[1]
-    nv = n_ex * v_rows
-    cs = nv // n_proj
+    picks = kc // reps
+    v_rows = v_ref.shape[0]
+    ep = flat.shape[0] // (sides * picks)
+    tokens = ex_dev * seq
 
     def peer(k):
         return lax.rem(me + k, n_proj)
 
-    def peer_ex(k):
-        return lax.rem(me_ex + k, n_ex)
-
-    others = [(a, b) for a in reversed(range(n_ex)) for b in range(n_proj) if (a, b) != (0, 0)]
     barrier = pltpu.get_barrier_semaphore()
-    for a, b in others:
-        pl.semaphore_signal(
-            barrier, inc=1, device_id=(grp, peer_ex(a), peer(b)), device_id_type=MESH
-        )
+
+    def greet(i, at):
+        pl.semaphore_signal(barrier, inc=1, device_id=(grp, i, at), device_id_type=MESH)
+
     loads = []
     for i, (src, dst) in enumerate(
         ((a_ref, ab), (x_ref, xb), (b_ref, bb), (c_ref, cb), (w_ref, wb))
@@ -296,12 +293,38 @@
         copy = pltpu.make_async_copy(src, dst, load_sem.at[i])
         copy.start()
         loads.append(copy)
-
-    def columns(at):
-        return v_ref.at[:, pl.ds(pl.multiple_of(at * width, 128), width)]
-
-    own = pltpu.make_async_copy(columns(me_ex), vals.at[me_ex], own_sem)
-    own.start()
+    for k in range(1, n_proj):
+        greet(me_ex, peer(k))
+    for i in range(1, n_ex):
+        @pl.when(i > me_ex)
+        def _():
+            greet(i, home * 2 + core)
+    for jj in range(2):
+        @pl.when(side * 2 + jj > me_ex)
+        def _():
+            for s in range(sides):
+                greet(side * 2 + jj, s * 2 + core)
+    expected = n_proj - 1 + me_ex + sides * jnp.clip(me_ex - 2 * side, 0, 2)
+
+    own = pltpu.make_async_copy(v_ref, held.at[side, pl.ds(slot * v_rows, v_rows)], own_sem)
+
+    @pl.when(home == side)
+    def _():
+        own.start()
+
+    def give(i):
+        return pltpu.make_async_remote_copy(
+            src_ref=v_ref, dst_ref=held.at[side, pl.ds(slot * v_rows, v_rows)],
+            send_sem=hs_sem.at[i], recv_sem=hr_sem.at[side, slot],
+            device_id=(grp, i, home * 2 + core), device_id_type=MESH,
+        )
+
+    def take(s, jj):
+        block = held.at[s, pl.ds(jj * v_rows, v_rows)]
+        return pltpu.make_async_remote_copy(
+            src_ref=block, dst_ref=block, send_sem=hs_sem.at[0], recv_sem=hr_sem.at[s, jj],
+            device_id=(grp, me_ex, me), device_id_type=MESH,
+        )
 
     def swap(k, src, dst, s_sem, r_sem):
         return pltpu.make_async_remote_copy(
@@ -309,17 +332,19 @@
             device_id=(grp, me_ex, peer(k)), device_id_type=MESH,
         )
 
-    def spread_out(src, dst, s_sem, r_sem):
-        started = []
-        for n, (a, b) in enumerate(others):
-            started.append(pltpu.make_async_remote_copy(
-                src_ref=src.at[peer_ex(a), peer(b)], dst_ref=dst.at[me_ex, me],
-                send_sem=s_sem.at[n], recv_sem=r_sem.at[n],
-                device_id=(grp, peer_ex(a), peer(b)), device_id_type=MESH,
-            ))
-            started[-1].start()
-        return started
-
+    @pl.when(me_ex > 0)
+    def _():
+        pl.semaphore_wait(barrier, expected)
+        for jj in range(2):
+            @pl.when(side * 2 + jj < me_ex)
+            def _():
+                for s in range(sides):
+                    pl.semaphore_signal(
+                        ready.at[me_ex], inc=1,
+                        device_id=(grp, side * 2 + jj, s * 2 + core), device_id_type=MESH,
+                    )
+
+    flat[...] = jnp.zeros_like(flat)
     loads[0].wait()
     m_in = dot(r_ref[0], ab[...]).astype(BF16)
     loads[1].wait()
@@ -331,140 +356,142 @@
     part = jnp.concatenate([part_in, part_out], axis=0)
     right_own[...] = part.astype(BF16)
 
-    pl.semaphore_wait(barrier, len(others))
-    copies = [swap(k, right_own, right_in, rs_sem, rr_sem) for k in range(1, n_proj)]
-    for copy in copies:
-        copy.start()
-    moves = []
-    for a in reversed(range(1, n_ex)):
-        moves.append(pltpu.make_async_remote_copy(
-            src_ref=columns(peer_ex(a)), dst_ref=vals.at[me_ex],
-            send_sem=gs_sem.at[a - 1], recv_sem=gr_sem.at[a - 1],
-            device_id=(grp, peer_ex(a), me), device_id_type=MESH,
-        ))
-        moves[-1].start()
-
-    loads[4].wait()
-    left[0] = dot(cb[...], wb[...]).astype(BF16)
-    left[1] = dot(xb[...], wb[...]).astype(BF16)
-
-    for copy in copies:
-        copy.wait()
-    total = part
-    for k in range(n_proj - 1):
-        total = total + right_in[k].astype(F32)
-    total = total.astype(BF16)
-
-    position = lax.broadcasted_iota(jnp.int32, (k2, seq), 1)
+    @pl.when(me_ex == 0)
+    def _():
+        pl.semaphore_wait(barrier, expected)
+
+    moves = [swap(k, right_own, right_in, rs_sem, rr_sem) for k in range(1, n_proj)]
+    for move in moves:
+        move.start()
+    for i in range(n_ex):
+        @pl.when((i < me_ex) | ((i == me_ex) & (home != side)))
+        def _():
+            give(i).start()
+
+    def give_later(k):
+        for i in range(k, n_ex):
+            @pl.when(i == me_ex + k)
+            def _():
+                pl.semaphore_wait(ready.at[i], 1)
+                give(i).start()
+
+    give_later(1)
+
+    position = lax.broadcasted_iota(jnp.int32, (k2, tokens), 1)
+    live = []
+    scale = []
     for e in range(ex_dev):
         count = len_ref[e]
-        live = position < count
-        for p in range(2):
-            piece = total[p * k2:(p + 1) * k2, e * seq:(e + 1) * seq].astype(F32)
-            piece = jnp.where(live, piece, 0.0).astype(BF16)
-            rows[e * pd + p * k2:e * pd + (p + 1) * k2, :] = (
-                dot(piece, left[p, e * seq:(e + 1) * seq, :]) / count.astype(F32)
-            )
-    group = lax.broadcasted_iota(jnp.int32, (pd, kc), 1) // sub
+        live.append((position >= e * seq) & (position < e * seq + count))
+        scale.append(1.0 / jnp.full((k2, 128), count.astype(F32), F32))
+
+    total = part
+    for k, move in enumerate(moves):
+        move.wait_recv()
+        total = total + right_in[k].astype(F32)
+    total = total.astype(BF16).astype(F32)
+    grown = []
+    for p, other in enumerate((cb, xb)):
+        piece = total[p * k2:(p + 1) * k2]
+        spread = jnp.concatenate([jnp.where(one, piece, 0.0) for one in live], axis=0).astype(BF16)
+        grown.append(dot(spread, other[...]))
+    loads[4].wait()
+    result = dot(jnp.concatenate(grown, axis=0).astype(BF16), wb[...])
+    for p in range(2):
+        for e in range(ex_dev):
+            at = (p * ex_dev + e) * k2
+            for q in range(n_proj):
+                rows[at:at + k2, q * kc:(q + 1) * kc] = result[at:at + k2, q * kc:(q + 1) * kc] * scale[e]
     for q in range(n_proj):
-        tiles = [rows[e * pd:(e + 1) * pd, q * kc:(q + 1) * kc] for e in range(ex_dev)]
-        for j in range(n_ex):
-            tile = jnp.zeros((pd, kc), F32)
-            for e in range(ex_dev):
-                shift = (e - j) * sub % kc
-                turned = pltpu.roll(tiles[e], shift, 1) if shift else tiles[e]
-                tile = jnp.where(group == e, turned, tile)
-            t_send[j, q] = tile.astype(BF16)
-    spreads = spread_out(t_send, t_recv, us_sem, ur_sem)
-    for j in range(n_proj):
-        t_own[j] = rows[:, j * kc:(j + 1) * kc].astype(BF16)
-    copies = [swap(k, t_own.at[peer(k)], t_in, ts_sem, tr_sem) for k in range(1, n_proj)]
-    for copy in copies:
-        copy.start()
-    t_recv[me_ex, me] = t_send[me_ex, me]
-
-    own.wait()
-    for move in moves:
-        move.wait()
-    held = vals[...].reshape(nv, width)
-    wide = held.astype(F32)
-    wide = wide * wide
-    acc = wide[:, :128]
-    for c in range(1, width // 128):
-        acc = acc + wide[:, c * 128:(c + 1) * 128]
-    val_sq = lax.dot_general(
-        jnp.ones((8, 128), F32), acc, NT,
-        precision=lax.Precision.HIGHEST, preferred_element_type=F32,
-    )[:1]
+        t_send[q % 2, q // 2] = rows[:, q * kc:(q + 1) * kc].astype(BF16)
+    shares = [
+        swap(k, t_send.at[lax.rem(peer(k), 2)], t_in, ts_sem, tr_sem) for k in range(1, n_proj)
+    ]
+    for share in shares:
+        share.start()
+    for k in range(2, n_ex):
+        give_later(k)
 
     l_at = lax.broadcasted_iota(jnp.int32, (128, kc), 0)
     k_at = lax.broadcasted_iota(jnp.int32, (128, kc), 1)
     keep = (k_at % reps) == (l_at // pd)
-    picks = kc // reps
     b_at = lax.broadcasted_iota(jnp.int32, (picks, kc), 0)
     s_at = lax.broadcasted_iota(jnp.int32, (picks, kc), 1)
     pick = jnp.where((s_at // reps) == b_at, 1.0, 0.0).astype(BF16)
 
-    def fan(one):
-        one = one.astype(BF16).astype(F32)
-        tiled = jnp.concatenate([one] * reps, axis=0)
-        return jnp.where(keep, tiled, 0.0).astype(BF16)
-
-    for copy in spreads:
-        copy.wait()
+    for s in range(sides):
+        for jj in range(2):
+            mine = (side * 2 + jj == me_ex) & (side == s)
+
+            @pl.when(mine)
+            def _():
+                own.wait()
+
+            @pl.when(jnp.logical_not(mine))
+            def _():
+                take(s, jj).wait_recv()
+    acc = jnp.zeros((2 * v_rows, 128), F32)
+    for s in range(sides):
+        for c in range(v_ref.shape[1] // 128):
+            wide = held[s, :, c * 128:(c + 1) * 128].astype(F32)
+            acc = acc + wide * wide
+    val_sq = lax.dot_general(
+        jnp.ones((ep, 128), F32), acc, NT, precision=lax.Precision.HIGHEST, preferred_element_type=F32
+    )
+
+    for share in shares:
+        share.wait_recv()
+    for s in range(sides):
+        block = rows[:, pl.ds(pl.multiple_of((s * 2 + core) * kc, 128), kc)]
+        for k in range(n_proj - 1):
+            block = block + t_in[k, s].astype(F32)
+        block = block.astype(BF16).astype(F32)
+        for e in range(ex_dev):
+            one = [block[(p * ex_dev + e) * k2:(p * ex_dev + e + 1) * k2] for p in range(2)]
+            tiled = jnp.where(keep, jnp.concatenate(one * reps, axis=0), 0.0)
+            shuf[(s * ex_dev + e) * 128:(s * ex_dev + e + 1) * 128, :] = tiled.astype(BF16)
+    spread = dot(pick, shuf[...], NT)
+    for s in range(sides):
+        for e in range(ex_dev):
+            flat[pl.ds(s * picks * ep + e, picks, stride=ep), :] = (
+                spread[:, (s * ex_dev + e) * 128:(s * ex_dev + e + 1) * 128]
+            )
+    dots = jnp.zeros((ep, 2 * v_rows), F32)
+    train_sq = jnp.zeros((ep, 128), F32)
+    for s in range(sides):
+        tiles = [flat[(s * picks + b) * ep:(s * picks + b + 1) * ep, :] for b in range(picks)]
+        for tile in tiles:
+            train_sq = train_sq + tile * tile
+        dots = dots + dot(jnp.concatenate(tiles, axis=1).astype(BF16), held[s], NT)
+    train_sq = jnp.sum(train_sq, axis=1, keepdims=True)
+    for jj in range(2):
+        span = slice(jj * v_rows, (jj + 1) * v_rows)
+        f_send[jj] = jnp.concatenate(
+            [dots[:, span], val_sq[:, span], jnp.broadcast_to(train_sq, (ep, 128 - 2 * v_rows))], axis=1
+        )
+    last = pltpu.make_async_remote_copy(
+        src_ref=f_send.at[1 - core], dst_ref=f_recv, send_sem=fs_sem, recv_sem=fr_sem,
+        device_id=(grp, me_ex, side * 2 + 1 - core), device_id_type=MESH,
+    )
+    last.start()
+
+    for b in range(picks):
+        tp_ref[:, b * 128:(b + 1) * 128] = flat[pl.ds(pl.multiple_of((side * picks + b) * ep, 8), ep), :]
+    for move in moves + shares:
+        move.wait_send()
     for i in range(n_ex):
-        one = t_recv[i, 0].astype(F32)
-        for p in range(1, n_proj):
-            one = one + t_recv[i, p].astype(F32)
-        shuf_all[i * 128:(i + 1) * 128, :] = fan(one)
-    spread = dot(pick, shuf_all[...], NT)
-    runs = width // 128
-    for i in range(n_ex):
-        for e in range(ex_dev):
-            for b in range(runs):
-                flat_all[i * ex_dev + e:i * ex_dev + e + 1, b * 128:(b + 1) * 128] = (
-                    spread[e * runs + b:e * runs + b + 1, i * 128:(i + 1) * 128]
-                )
-    train = flat_all[...]
-    train_sq = jnp.sum(train * train, axis=1, keepdims=True)
-    dots = dot(train.astype(BF16), held, NT)
-    every = n_ex * ex_dev
-    for q in range(n_proj):
-        packed = jnp.concatenate([
-            dots[:, q * cs:(q + 1) * cs],
-            jnp.broadcast_to(val_sq[:, q * cs:(q + 1) * cs], (every, cs)),
-            jnp.broadcast_to(train_sq, (every, 128 - 2 * cs)),
-        ], axis=1)
-        for i in range(n_ex):
-            f_send[i, q] = packed[i * ex_dev:(i + 1) * ex_dev]
-    spreads = spread_out(f_send, f_recv, fs_sem, fr_sem)
-    f_recv[me_ex, me] = f_send[me_ex, me]
-
-    mine = rows[:, pl.ds(pl.multiple_of(me * kc, 128), kc)]
-    for copy in copies:
-        copy.wait()
-    for k in range(n_proj - 1):
-        mine = mine + t_in[k].astype(F32)
-    for e in range(ex_dev):
-        shuf[e * 128:(e + 1) * 128, :] = fan(mine[e * pd:(e + 1) * pd, :])
-    spread = dot(pick, shuf[...], NT)
-    for b in range(picks):
-        for e in range(ex_dev):
-            tp_ref[e:e + 1, b * 128:(b + 1) * 128] = spread[b:b + 1, e * 128:(e + 1) * 128]
-
-    for copy in spreads:
-        copy.wait()
-    final = jnp.zeros(f_recv.shape[2:], F32)
-    for i in range(n_ex):
-        for p in range(n_proj):
-            final = final + f_recv[i, p]
-    sc_ref[...] = final
-
-
-def near_finish(pdim, train_ref, sums_ref, tp_ref, sc_ref):
+        @pl.when((i != me_ex) | (home != side))
+        def _():
+            give(i).wait_send()
+    final = f_send[core]
+    last.wait()
+    sc_ref[...] = final + f_recv[...]
+
+
+def paired_finish(pdim, train_ref, sums_ref, tp_ref, sc_ref):
     ex_dev, cs = sc_ref.shape
     tp_ref[...] = train_ref[:ex_dev, :].astype(BF16)
-    final = sums_ref[...]
+    final = sums_ref[:ex_dev, :]
     sc_ref[...] = (
         math.sqrt(pdim)
         * final[:, :cs]
@@ -508,10 +535,10 @@
     vmem = pl.BlockSpec(memory_space=pltpu.VMEM)
     dma = pltpu.SemaphoreType.DMA
     peers = n_proj - 1
-    sub = kc // n_ex
-    near = (
-        kc == 128 and sub * n_ex == kc and sub * ex_dev == 128 and sub * pd % 128 == 0
-        and nv % 128 == 0 and 3 * cs <= 128
+    sides = n_proj // 2
+    paired = (
+        n_ex == n_proj and n_proj % 2 == 0 and kc == 128 and 3 * v_rows <= 128 and v_rows % 16 == 0
+        and k2 == 8 and ex_dev <= ep and v_cols == kc * pd
     )
     head = [
         pltpu.VMEM((tokens, cols), BF16),
@@ -519,39 +546,36 @@
         pltpu.VMEM((rank, cols), BF16),
         pltpu.VMEM((cols, rank), BF16),
         pltpu.VMEM((cols, k1), BF16),
-        pltpu.VMEM((ex_dev * pd, k1), F32),
-        pltpu.VMEM((2, tokens, k1), BF16),
     ]
-    if near:
-        rest = n_ex * n_proj - 1
-        body, end = near_kernel, near_finish
-        sums_shape = (ex_dev, 128)
+    if paired:
+        body, end = paired_kernel, paired_finish
+        sums_shape = (ep, 128)
+        picks = kc * pd // 128
         scratch = head + [
-            pltpu.VMEM((n_ex, v_rows, sub * pd), BF16),
+            pltpu.VMEM((sides, 2 * v_rows, v_cols), BF16),
+            pltpu.VMEM((ex_dev * pd, k1), F32),
             pltpu.VMEM((pd, tokens), BF16),
             pltpu.VMEM((peers, pd, tokens), BF16),
-            pltpu.VMEM((n_proj, ex_dev * pd, kc), BF16),
-            pltpu.VMEM((peers, ex_dev * pd, kc), BF16),
-            pltpu.VMEM((n_ex, n_proj, pd, kc), BF16),
-            pltpu.VMEM((n_ex, n_proj, pd, kc), BF16),
-            pltpu.VMEM((ex_dev * 128, kc), BF16),
-            pltpu.VMEM((n_ex * 128, kc), BF16),
-            pltpu.VMEM((n_ex * ex_dev, sub * pd), F32),
-            pltpu.VMEM((n_ex, n_proj, ex_dev, 128), F32),
-            pltpu.VMEM((n_ex, n_proj, ex_dev, 128), F32),
+            pltpu.VMEM((2, sides, ex_dev * pd, kc), BF16),
+            pltpu.VMEM((peers, sides, ex_dev * pd, kc), BF16),
+            pltpu.VMEM((sides * ex_dev * 128, kc), BF16),
+            pltpu.VMEM((sides * picks * ep, 128), F32),
+            pltpu.VMEM((2, ep, 128), F32),
+            pltpu.VMEM((ep, 128), F32),
             dma((5,)),
             dma((peers,)), dma((peers,)),
             dma((peers,)), dma((peers,)),
-            dma((rest,)), dma((rest,)),
-            dma((rest,)), dma((rest,)),
-            dma((n_ex - 1,)), dma((n_ex - 1,)),
-            dma,
+            dma((n_ex,)), dma((sides, 2)),
+            dma, dma, dma,
+            pltpu.SemaphoreType.REGULAR((n_ex,)),
         ]
     else:
         chunks = 2 if v_rows % 32 == 0 else 1
         body, end = kernel, finish
         sums_shape = (2 * ep + 8, cs)
         scratch = head + [
+            pltpu.VMEM((ex_dev * pd, k1), F32),
+            pltpu.VMEM((2, tokens, k1), BF16),
             pltpu.VMEM((n_ex, v_rows, v_cols), BF16),
             pltpu.VMEM((pd, tokens), BF16),
             pltpu.VMEM((peers, pd, tokens), BF16),

time: 20.5 us -> 22.5 us (1.098)
  the two profiles are of different devices: /device:TPU:0 before, /device:TPU:25 now
where the time goes in v1:
time: 22.5 us; the launch traced here: 22.3 us
  Pallas kernels  21.7 us (96%)
  between operations  0.64 us (3%)
    pallas_call x1, Pallas kernels, shards(): pl.pallas_call(functools.partial(body, (n_ex, n_proj, ex_dev, seq, pdim))...  21 us
    pallas_call x1, Pallas kernels, shards(): pl.pallas_call(functools.partial(end, pdim), out_shape=(jax.ShapeDtypeStr...  0.66 us

profile of v1, /device:TPU:25, one launch (start us, length us, event | category | flops | bytes accessed | tf_op | source)
XLA Modules:
  0.0 22.3 jit_solution(1357819012429756609)
XLA Ops:
  0.6 21.0 %project.1 = (f32[8,2048]{1,0:T(8,128)S(1)}, f32[8,128]{1,0:T(8,128)S(1)}) custom-call(s32[4]{0:T(128)} %len_ref.1, bf16[576,1280]{1,0:T(8,128)(2,1)} %bitcast.3, bf16[576,1280]{1,0:T(8,128)(2,1)} %bitcast.4, bf16[128,1280]{1,0:T(8,128)(2,1)} %a_ref.1, bf16[1280,128]{1,0:T(8,128)(2,1)} %b_ref.1, bf16[1280,512]{1,0:T(8,128)(2,1)} %w_ref.1, ...), custom_call_target="tpu_custom_call" | custom-call | tf_op jit(solution)/shard_map/project/pallas_call | solution.py:596
  21.7 0.7 %finish.1 = (bf16[4,2048]{1,0:T(4,128)(2,1)}, f32[4,32]{1,0:T(4,128)}) custom-call(f32[8,2048]{1,0:T(8,128)S(1)} %get-tuple-element.4.train_ref, f32[8,128]{1,0:T(8,128)S(1)} %get-tuple-element.5.sums_ref), custom_call_target="tpu_custom_call" | custom-call | tf_op jit(solution)/shard_map/finish/pallas_call | solution.py:614

commit v2 on v1

--- a/solution.py
+++ b/solution.py
@@ -259,23 +259,24 @@
 
 def paired_kernel(
     sizes,
-    len_ref, x_ref, c_ref, a_ref, b_ref, w_ref, r_ref, v_ref,
+    len_hbm, x_ref, c_ref, a_ref, b_ref, w_ref, r_hbm, v_ref,
     tp_ref, sc_ref,
-    xb, cb, ab, bb, wb, held, rows, right_own, right_in, t_send, t_in, shuf, flat, f_send, f_recv,
-    load_sem, rs_sem, rr_sem, ts_sem, tr_sem, hs_sem, hr_sem, fs_sem, fr_sem, own_sem, ready,
+    xb, cb, ab, bb, wb, r_ref, len_ref, held, rows, right_own, right_in, t_send, t_in, t_mate, shuf, flat, f_send, f_recv,
+    load_sem, rs_sem, rr_sem, ts_sem, tr_sem, us_sem, ur_sem, hs_sem, hr_sem, fs_sem, fr_sem, own_sem, ready, met,
 ):
     n_ex, n_proj, ex_dev, seq, pdim = sizes
     grp, me_ex, me = lax.axis_index("grp"), lax.axis_index("ex"), lax.axis_index("proj")
-    side, core = me // 2, lax.rem(me, 2)
-    home, slot = me_ex // 2, lax.rem(me_ex, 2)
-    sides = n_proj // 2
+    flank = lax.rem(me_ex, 2)
+    mate = me_ex + 1 - 2 * flank
+    per = n_ex // 2
+    home, slot = me_ex // per, lax.rem(me_ex, per)
     k2 = r_ref.shape[1]
     pd = 2 * k2
     kc = wb.shape[1] // n_proj
     reps = 128 // pd
     picks = kc // reps
     v_rows = v_ref.shape[0]
-    ep = flat.shape[0] // (sides * picks)
+    ep = flat.shape[1] // picks
     tokens = ex_dev * seq
 
     def peer(k):
@@ -288,7 +289,7 @@
 
     loads = []
     for i, (src, dst) in enumerate(
-        ((a_ref, ab), (x_ref, xb), (b_ref, bb), (c_ref, cb), (w_ref, wb))
+        ((r_hbm, r_ref), (a_ref, ab), (x_ref, xb), (b_ref, bb), (c_ref, cb), (w_ref, wb), (len_hbm, len_ref))
     ):
         copy = pltpu.make_async_copy(src, dst, load_sem.at[i])
         copy.start()
@@ -298,32 +299,39 @@
     for i in range(1, n_ex):
         @pl.when(i > me_ex)
         def _():
-            greet(i, home * 2 + core)
-    for jj in range(2):
-        @pl.when(side * 2 + jj > me_ex)
-        def _():
-            for s in range(sides):
-                greet(side * 2 + jj, s * 2 + core)
-    expected = n_proj - 1 + me_ex + sides * jnp.clip(me_ex - 2 * side, 0, 2)
-
-    own = pltpu.make_async_copy(v_ref, held.at[side, pl.ds(slot * v_rows, v_rows)], own_sem)
-
-    @pl.when(home == side)
+            greet(i, me)
+
+    @pl.when(flank == 0)
+    def _():
+        for k in range(1, n_proj):
+            greet(mate, peer(k))
+    expected = n_proj - 1 + me_ex + flank * (n_proj - 1)
+
+    def place(jj):
+        return held.at[pl.ds(jj * v_rows, v_rows)]
+
+    own = pltpu.make_async_copy(v_ref, place(slot), own_sem)
+
+    @pl.when(home == flank)
     def _():
         own.start()
 
     def give(i):
         return pltpu.make_async_remote_copy(
-            src_ref=v_ref, dst_ref=held.at[side, pl.ds(slot * v_rows, v_rows)],
-            send_sem=hs_sem.at[i], recv_sem=hr_sem.at[side, slot],
-            device_id=(grp, i, home * 2 + core), device_id_type=MESH,
-        )
-
-    def take(s, jj):
-        block = held.at[s, pl.ds(jj * v_rows, v_rows)]
-        return pltpu.make_async_remote_copy(
-            src_ref=block, dst_ref=block, send_sem=hs_sem.at[0], recv_sem=hr_sem.at[s, jj],
+            src_ref=v_ref, dst_ref=place(slot), send_sem=hs_sem.at[i], recv_sem=hr_sem.at[slot],
+            device_id=(grp, i, me), device_id_type=MESH,
+        )
+
+    def take(jj):
+        return pltpu.make_async_remote_copy(
+            src_ref=place(jj), dst_ref=place(jj), send_sem=hs_sem.at[0], recv_sem=hr_sem.at[jj],
             device_id=(grp, me_ex, me), device_id_type=MESH,
+        )
+
+    def pass_on(k, src, dst, s_sem, r_sem):
+        return pltpu.make_async_remote_copy(
+            src_ref=src, dst_ref=dst.at[k], send_sem=s_sem.at[k], recv_sem=r_sem.at[k],
+            device_id=(grp, mate, peer(k)), device_id_type=MESH,
         )
 
     def swap(k, src, dst, s_sem, r_sem):
@@ -335,23 +343,29 @@
     @pl.when(me_ex > 0)
     def _():
         pl.semaphore_wait(barrier, expected)
-        for jj in range(2):
-            @pl.when(side * 2 + jj < me_ex)
+        for j in range(n_ex - 1):
+            @pl.when((j < me_ex) & (j // per == flank))
             def _():
-                for s in range(sides):
-                    pl.semaphore_signal(
-                        ready.at[me_ex], inc=1,
-                        device_id=(grp, side * 2 + jj, s * 2 + core), device_id_type=MESH,
-                    )
+                pl.semaphore_signal(
+                    ready.at[me_ex], inc=1, device_id=(grp, j, me), device_id_type=MESH
+                )
+
+        @pl.when(flank == 1)
+        def _():
+            for k in range(n_proj):
+                pl.semaphore_signal(
+                    met, inc=1, device_id=(grp, mate, peer(k)), device_id_type=MESH
+                )
 
     flat[...] = jnp.zeros_like(flat)
     loads[0].wait()
+    loads[1].wait()
     m_in = dot(r_ref[0], ab[...]).astype(BF16)
-    loads[1].wait()
+    loads[2].wait()
     part_in = dot(m_in, xb[...], NT)
-    loads[2].wait()
+    loads[3].wait()
     m_out = dot(r_ref[1], bb[...], NT).astype(BF16)
-    loads[3].wait()
+    loads[4].wait()
     part_out = dot(m_out, cb[...], NT)
     part = jnp.concatenate([part_in, part_out], axis=0)
     right_own[...] = part.astype(BF16)
@@ -363,20 +377,21 @@
     moves = [swap(k, right_own, right_in, rs_sem, rr_sem) for k in range(1, n_proj)]
     for move in moves:
         move.start()
-    for i in range(n_ex):
-        @pl.when((i < me_ex) | ((i == me_ex) & (home != side)))
+    for i in range(n_ex - 1):
+        @pl.when((i < me_ex) & (i % 2 == home))
         def _():
             give(i).start()
 
     def give_later(k):
         for i in range(k, n_ex):
-            @pl.when(i == me_ex + k)
+            @pl.when((i == me_ex + k) & (i % 2 == home))
             def _():
                 pl.semaphore_wait(ready.at[i], 1)
                 give(i).start()
 
     give_later(1)
 
+    loads[6].wait()
     position = lax.broadcasted_iota(jnp.int32, (k2, tokens), 1)
     live = []
     scale = []
@@ -395,7 +410,7 @@
         piece = total[p * k2:(p + 1) * k2]
         spread = jnp.concatenate([jnp.where(one, piece, 0.0) for one in live], axis=0).astype(BF16)
         grown.append(dot(spread, other[...]))
-    loads[4].wait()
+    loads[5].wait()
     result = dot(jnp.concatenate(grown, axis=0).astype(BF16), wb[...])
     for p in range(2):
         for e in range(ex_dev):
@@ -403,11 +418,17 @@
             for q in range(n_proj):
                 rows[at:at + k2, q * kc:(q + 1) * kc] = result[at:at + k2, q * kc:(q + 1) * kc] * scale[e]
     for q in range(n_proj):
-        t_send[q % 2, q // 2] = rows[:, q * kc:(q + 1) * kc].astype(BF16)
-    shares = [
-        swap(k, t_send.at[lax.rem(peer(k), 2)], t_in, ts_sem, tr_sem) for k in range(1, n_proj)
-    ]
+        t_send[q] = rows[:, q * kc:(q + 1) * kc].astype(BF16)
+    shares = [swap(k, t_send.at[peer(k)], t_in, ts_sem, tr_sem) for k in range(1, n_proj)]
     for share in shares:
+        share.start()
+
+    @pl.when(flank == 0)
+    def _():
+        pl.semaphore_wait(met, n_proj)
+
+    across = [pass_on(k, t_send.at[peer(k)], t_mate, us_sem, ur_sem) for k in range(n_proj)]
+    for share in across:
         share.start()
     for k in range(2, n_ex):
         give_later(k)
@@ -419,73 +440,100 @@
     s_at = lax.broadcasted_iota(jnp.int32, (picks, kc), 1)
     pick = jnp.where((s_at // reps) == b_at, 1.0, 0.0).astype(BF16)
 
-    for s in range(sides):
-        for jj in range(2):
-            mine = (side * 2 + jj == me_ex) & (side == s)
-
-            @pl.when(mine)
-            def _():
-                own.wait()
-
-            @pl.when(jnp.logical_not(mine))
-            def _():
-                take(s, jj).wait_recv()
-    acc = jnp.zeros((2 * v_rows, 128), F32)
-    for s in range(sides):
-        for c in range(v_ref.shape[1] // 128):
-            wide = held[s, :, c * 128:(c + 1) * 128].astype(F32)
-            acc = acc + wide * wide
+    for jj in range(per):
+        @pl.when(flank * per + jj == me_ex)
+        def _():
+            own.wait()
+
+        @pl.when(flank * per + jj != me_ex)
+        def _():
+            take(jj).wait_recv()
+    acc = jnp.zeros((per * v_rows, 128), F32)
+    for c in range(v_ref.shape[1] // 128):
+        wide = held[:, c * 128:(c + 1) * 128].astype(F32)
+        acc = acc + wide * wide
     val_sq = lax.dot_general(
         jnp.ones((ep, 128), F32), acc, NT, precision=lax.Precision.HIGHEST, preferred_element_type=F32
     )
 
-    for share in shares:
-        share.wait_recv()
-    for s in range(sides):
-        block = rows[:, pl.ds(pl.multiple_of((s * 2 + core) * kc, 128), kc)]
-        for k in range(n_proj - 1):
-            block = block + t_in[k, s].astype(F32)
+    def score(w, block):
         block = block.astype(BF16).astype(F32)
         for e in range(ex_dev):
             one = [block[(p * ex_dev + e) * k2:(p * ex_dev + e + 1) * k2] for p in range(2)]
             tiled = jnp.where(keep, jnp.concatenate(one * reps, axis=0), 0.0)
-            shuf[(s * ex_dev + e) * 128:(s * ex_dev + e + 1) * 128, :] = tiled.astype(BF16)
-    spread = dot(pick, shuf[...], NT)
-    for s in range(sides):
+            shuf[w, e * 128:(e + 1) * 128, :] = tiled.astype(BF16)
+        spread = dot(pick, shuf[w], NT)
         for e in range(ex_dev):
-            flat[pl.ds(s * picks * ep + e, picks, stride=ep), :] = (
-                spread[:, (s * ex_dev + e) * 128:(s * ex_dev + e + 1) * 128]
-            )
-    dots = jnp.zeros((ep, 2 * v_rows), F32)
-    train_sq = jnp.zeros((ep, 128), F32)
-    for s in range(sides):
-        tiles = [flat[(s * picks + b) * ep:(s * picks + b + 1) * ep, :] for b in range(picks)]
+            flat[w, pl.ds(e, picks, stride=ep), :] = spread[:, e * 128:(e + 1) * 128]
+        tiles = [flat[w, b * ep:(b + 1) * ep, :] for b in range(picks)]
+        train_sq = jnp.zeros((ep, 128), F32)
         for tile in tiles:
             train_sq = train_sq + tile * tile
-        dots = dots + dot(jnp.concatenate(tiles, axis=1).astype(BF16), held[s], NT)
-    train_sq = jnp.sum(train_sq, axis=1, keepdims=True)
-    for jj in range(2):
-        span = slice(jj * v_rows, (jj + 1) * v_rows)
-        f_send[jj] = jnp.concatenate(
-            [dots[:, span], val_sq[:, span], jnp.broadcast_to(train_sq, (ep, 128 - 2 * v_rows))], axis=1
-        )
-    last = pltpu.make_async_remote_copy(
-        src_ref=f_send.at[1 - core], dst_ref=f_recv, send_sem=fs_sem, recv_sem=fr_sem,
-        device_id=(grp, me_ex, side * 2 + 1 - core), device_id_type=MESH,
-    )
-    last.start()
-
-    for b in range(picks):
-        tp_ref[:, b * 128:(b + 1) * 128] = flat[pl.ds(pl.multiple_of((side * picks + b) * ep, 8), ep), :]
-    for move in moves + shares:
+        train_sq = jnp.sum(train_sq, axis=1, keepdims=True)
+        train = jnp.concatenate(tiles, axis=1)
+        dots = dot(train.astype(BF16), held[...], NT)
+        for jj in range(per):
+            span = slice(jj * v_rows, (jj + 1) * v_rows)
+            f_send[w, jj] = jnp.concatenate(
+                [dots[:, span], val_sq[:, span], jnp.broadcast_to(train_sq, (ep, 128 - 2 * v_rows))],
+                axis=1,
+            )
+        return train
+
+    def report(w, jj):
+        return pltpu.make_async_remote_copy(
+            src_ref=f_send.at[w, jj], dst_ref=f_recv.at[me], send_sem=fs_sem.at[w, jj], recv_sem=fr_sem.at[me],
+            device_id=(grp, mate if w else me_ex, flank * per + jj), device_id_type=MESH,
+        )
+
+    def hear(q):
+        return pltpu.make_async_remote_copy(
+            src_ref=f_recv.at[q], dst_ref=f_recv.at[q], send_sem=fs_sem.at[0, 0], recv_sem=fr_sem.at[q],
+            device_id=(grp, me_ex, me), device_id_type=MESH,
+        )
+
+    block = rows[:, pl.ds(pl.multiple_of(me * kc, 128), kc)]
+    for k, share in enumerate(shares):
+        share.wait_recv()
+        block = block + t_in[k].astype(F32)
+    train = score(0, block)
+    for jj in range(per):
+        @pl.when(me != flank * per + jj)
+        def _():
+            report(0, jj).start()
+
+        @pl.when(me == flank * per + jj)
+        def _():
+            f_recv[me] = f_send[0, jj]
+    block = jnp.zeros((ex_dev * pd, kc), F32)
+    for k, share in enumerate(across):
+        share.wait_recv()
+        block = block + t_mate[k].astype(F32)
+    score(1, block)
+    for jj in range(per):
+        report(1, jj).start()
+
+    tp_ref[...] = train
+    for move in moves + shares + across:
         move.wait_send()
     for i in range(n_ex):
-        @pl.when((i != me_ex) | (home != side))
+        @pl.when((i != me_ex) & (i % 2 == home))
         def _():
             give(i).wait_send()
-    final = f_send[core]
-    last.wait()
-    sc_ref[...] = final + f_recv[...]
+    for q in range(n_proj):
+        @pl.when((me // per != flank) | (me != q))
+        def _():
+            hear(q).wait_recv()
+    final = f_recv[0]
+    for q in range(1, n_proj):
+        final = final + f_recv[q]
+    sc_ref[...] = final
+    for jj in range(per):
+        @pl.when(me != flank * per + jj)
+        def _():
+            report(0, jj).wait_send()
+
+        report(1, jj).wait_send()
 
 
 def paired_finish(pdim, train_ref, sums_ref, tp_ref, sc_ref):
@@ -535,10 +583,10 @@
     vmem = pl.BlockSpec(memory_space=pltpu.VMEM)
     dma = pltpu.SemaphoreType.DMA
     peers = n_proj - 1
-    sides = n_proj // 2
+    per = n_ex // 2
     paired = (
-        n_ex == n_proj and n_proj % 2 == 0 and kc == 128 and 3 * v_rows <= 128 and v_rows % 16 == 0
-        and k2 == 8 and ex_dev <= ep and v_cols == kc * pd
+        n_ex == n_proj and n_ex % 2 == 0 and kc == 128 and 3 * v_rows <= 128 and v_rows % 16 == 0
+        and k2 % 8 == 0 and v_cols == kc * pd
     )
     head = [
         pltpu.VMEM((tokens, cols), BF16),
@@ -551,25 +599,33 @@
         body, end = paired_kernel, paired_finish
         sums_shape = (ep, 128)
         picks = kc * pd // 128
+        firsts = [any_space] * 8
         scratch = head + [
-            pltpu.VMEM((sides, 2 * v_rows, v_cols), BF16),
+            pltpu.VMEM((2, k2, rank), BF16),
+            pltpu.SMEM((ex_dev,), jnp.int32),
+            pltpu.VMEM((per * v_rows, v_cols), BF16),
             pltpu.VMEM((ex_dev * pd, k1), F32),
             pltpu.VMEM((pd, tokens), BF16),
             pltpu.VMEM((peers, pd, tokens), BF16),
-            pltpu.VMEM((2, sides, ex_dev * pd, kc), BF16),
-            pltpu.VMEM((peers, sides, ex_dev * pd, kc), BF16),
-            pltpu.VMEM((sides * ex_dev * 128, kc), BF16),
-            pltpu.VMEM((sides * picks * ep, 128), F32),
-            pltpu.VMEM((2, ep, 128), F32),
-            pltpu.VMEM((ep, 128), F32),
-            dma((5,)),
+            pltpu.VMEM((n_proj, ex_dev * pd, kc), BF16),
+            pltpu.VMEM((peers, ex_dev * pd, kc), BF16),
+            pltpu.VMEM((n_proj, ex_dev * pd, kc), BF16),
+            pltpu.VMEM((2, ex_dev * 128, kc), BF16),
+            pltpu.VMEM((2, picks * ep, 128), F32),
+            pltpu.VMEM((2, per, ep, 128), F32),
+            pltpu.VMEM((n_proj, ep, 128), F32),
+            dma((7,)),
             dma((peers,)), dma((peers,)),
             dma((peers,)), dma((peers,)),
-            dma((n_ex,)), dma((sides, 2)),
-            dma, dma, dma,
+            dma((n_proj,)), dma((n_proj,)),
+            dma((n_ex,)), dma((per,)),
+            dma((2, per)), dma((n_proj,)),
+            dma,
             pltpu.SemaphoreType.REGULAR((n_ex,)),
+            pltpu.SemaphoreType.REGULAR,
         ]
     else:
+        firsts = [pl.BlockSpec(memory_space=pltpu.SMEM)] + [any_space] * 5 + [vmem, any_space]
         chunks = 2 if v_rows % 32 == 0 else 1
         body, end = kernel, finish
         sums_shape = (2 * ep + 8, cs)
@@ -599,7 +655,7 @@
             pltpu.VMEM((ep, v_cols), F32),
             pltpu.VMEM(sums_shape, F32),
         ),
-        in_specs=[pl.BlockSpec(memory_space=pltpu.SMEM)] + [any_space] * 5 + [vmem, any_space],
+        in_specs=firsts,
         out_specs=(vmem, vmem),
         scratch_shapes=scratch,
         compiler_params=pltpu.CompilerParams(

time: 22.5 us -> 18.1 us (0.80)
  Pallas kernels: 21.7 us -> 17.2 us
    pallas_call x1, Pallas kernels: 21 us -> 16.6 us  [shards(): pl.pallas_call(functools.partial(body, (n_ex, n_proj, ex_dev, seq, pdim))...]
where the time goes in v2:
time: 18.1 us; the launch traced here: 17.9 us
  Pallas kernels  17.2 us (95%)
  between operations  0.64 us (4%)
    pallas_call x1, Pallas kernels, shards(): pl.pallas_call(functools.partial(body, (n_ex, n_proj, ex_dev, seq, pdim))...  16.6 us
    pallas_call x1, Pallas kernels, shards(): pl.pallas_call(functools.partial(end, pdim), out_shape=(jax.ShapeDtypeStr...  0.66 us

profile of v2, /device:TPU:25, one launch (start us, length us, event | category | flops | bytes accessed | tf_op | source)
XLA Modules:
  0.0 17.9 jit_solution(3220371233502393763)
XLA Ops:
  0.6 16.6 %project.1 = (f32[8,2048]{1,0:T(8,128)S(1)}, f32[8,128]{1,0:T(8,128)S(1)}) custom-call(s32[4]{0:T(128)} %len_hbm.1, bf16[576,1280]{1,0:T(8,128)(2,1)} %bitcast.3, bf16[576,1280]{1,0:T(8,128)(2,1)} %bitcast.4, bf16[128,1280]{1,0:T(8,128)(2,1)} %a_ref.1, bf16[1280,128]{1,0:T(8,128)(2,1)} %b_ref.1, bf16[1280,512]{1,0:T(8,128)(2,1)} %w_ref.1, ...), custom_call_target="tpu_custom_call" | custom-call | tf_op jit(solution)/shard_map/project/pallas_call | solution.py:652
  17.2 0.7 %finish.1 = (bf16[4,2048]{1,0:T(4,128)(2,1)}, f32[4,32]{1,0:T(4,128)}) custom-call(f32[8,2048]{1,0:T(8,128)S(1)} %get-tuple-element.4.train_ref, f32[8,128]{1,0:T(8,128)S(1)} %get-tuple-element.5.sums_ref), custom_call_target="tpu_custom_call" | custom-call | tf_op jit(solution)/shard_map/finish/pallas_call | solution.py:670

commit v3 on v2

--- a/solution.py
+++ b/solution.py
@@ -350,6 +350,11 @@
                     ready.at[me_ex], inc=1, device_id=(grp, j, me), device_id_type=MESH
                 )
 
+        for i in range(n_ex - 1):
+            @pl.when((i < me_ex) & (i % 2 == home))
+            def _():
+                give(i).start()
+
         @pl.when(flank == 1)
         def _():
             for k in range(n_proj):
@@ -377,11 +382,6 @@
     moves = [swap(k, right_own, right_in, rs_sem, rr_sem) for k in range(1, n_proj)]
     for move in moves:
         move.start()
-    for i in range(n_ex - 1):
-        @pl.when((i < me_ex) & (i % 2 == home))
-        def _():
-            give(i).start()
-
     def give_later(k):
         for i in range(k, n_ex):
             @pl.when((i == me_ex + k) & (i % 2 == home))
@@ -389,7 +389,8 @@
                 pl.semaphore_wait(ready.at[i], 1)
                 give(i).start()
 
-    give_later(1)
+    for k in range(1, n_ex):
+        give_later(k)
 
     loads[6].wait()
     position = lax.broadcasted_iota(jnp.int32, (k2, tokens), 1)
@@ -430,8 +431,6 @@
     across = [pass_on(k, t_send.at[peer(k)], t_mate, us_sem, ur_sem) for k in range(n_proj)]
     for share in across:
         share.start()
-    for k in range(2, n_ex):
-        give_later(k)
 
     l_at = lax.broadcasted_iota(jnp.int32, (128, kc), 0)
     k_at = lax.broadcasted_iota(jnp.int32, (128, kc), 1)

time: 18.1 us -> 16.6 us (0.917)
  Pallas kernels: 17.2 us -> 15.8 us
    pallas_call x1, Pallas kernels: 16.6 us -> 15.2 us  [shards(): pl.pallas_call(functools.partial(body, (n_ex, n_proj, ex_dev, seq, pdim))...]
where the time goes in v3:
time: 16.6 us; the launch traced here: 16.5 us
  Pallas kernels  15.8 us (95%)
  between operations  0.64 us (4%)
    pallas_call x1, Pallas kernels, shards(): pl.pallas_call(functools.partial(body, (n_ex, n_proj, ex_dev, seq, pdim))...  15.2 us
    pallas_call x1, Pallas kernels, shards(): pl.pallas_call(functools.partial(end, pdim), out_shape=(jax.ShapeDtypeStr...  0.66 us

profile of v3, /device:TPU:25, one launch (start us, length us, event | category | flops | bytes accessed | tf_op | source)
XLA Modules:
  0.0 16.5 jit_solution(975658187965268748)
XLA Ops:
  0.6 15.2 %project.1 = (f32[8,2048]{1,0:T(8,128)S(1)}, f32[8,128]{1,0:T(8,128)S(1)}) custom-call(s32[4]{0:T(128)} %len_hbm.1, bf16[576,1280]{1,0:T(8,128)(2,1)} %bitcast.3, bf16[576,1280]{1,0:T(8,128)(2,1)} %bitcast.4, bf16[128,1280]{1,0:T(8,128)(2,1)} %a_ref.1, bf16[1280,128]{1,0:T(8,128)(2,1)} %b_ref.1, bf16[1280,512]{1,0:T(8,128)(2,1)} %w_ref.1, ...), custom_call_target="tpu_custom_call" | custom-call | tf_op jit(solution)/shard_map/project/pallas_call | solution.py:651
  15.8 0.7 %finish.1 = (bf16[4,2048]{1,0:T(4,128)(2,1)}, f32[4,32]{1,0:T(4,128)}) custom-call(f32[8,2048]{1,0:T(8,128)S(1)} %get-tuple-element.4.train_ref, f32[8,128]{1,0:T(8,128)S(1)} %get-tuple-element.5.sums_ref), custom_call_target="tpu_custom_call" | custom-call | tf_op jit(solution)/shard_map/finish/pallas_call | solution.py:669

commit v4 on v3

--- a/solution.py
+++ b/solution.py
@@ -289,7 +289,7 @@
 
     loads = []
     for i, (src, dst) in enumerate(
-        ((r_hbm, r_ref), (a_ref, ab), (x_ref, xb), (b_ref, bb), (c_ref, cb), (w_ref, wb), (len_hbm, len_ref))
+        ((r_hbm, r_ref), (a_ref, ab), (b_ref, bb), (x_ref, xb), (c_ref, cb), (w_ref, wb), (len_hbm, len_ref))
     ):
         copy = pltpu.make_async_copy(src, dst, load_sem.at[i])
         copy.start()
@@ -340,6 +340,11 @@
             device_id=(grp, me_ex, peer(k)), device_id_type=MESH,
         )
 
+    flat[...] = jnp.zeros_like(flat)
+    for copy in loads[:3]:
+        copy.wait()
+    m_in = dot(r_ref[0], ab[...]).astype(BF16)
+    m_out = dot(r_ref[1], bb[...], NT).astype(BF16)
     @pl.when(me_ex > 0)
     def _():
         pl.semaphore_wait(barrier, expected)
@@ -362,14 +367,8 @@
                     met, inc=1, device_id=(grp, mate, peer(k)), device_id_type=MESH
                 )
 
-    flat[...] = jnp.zeros_like(flat)
-    loads[0].wait()
-    loads[1].wait()
-    m_in = dot(r_ref[0], ab[...]).astype(BF16)
-    loads[2].wait()
+    loads[3].wait()
     part_in = dot(m_in, xb[...], NT)
-    loads[3].wait()
-    m_out = dot(r_ref[1], bb[...], NT).astype(BF16)
     loads[4].wait()
     part_out = dot(m_out, cb[...], NT)
     part = jnp.concatenate([part_in, part_out], axis=0)
@@ -421,16 +420,21 @@
     for q in range(n_proj):
         t_send[q] = rows[:, q * kc:(q + 1) * kc].astype(BF16)
     shares = [swap(k, t_send.at[peer(k)], t_in, ts_sem, tr_sem) for k in range(1, n_proj)]
+    across = [pass_on(k, t_send.at[peer(k)], t_mate, us_sem, ur_sem) for k in range(n_proj)]
+
+    @pl.when(flank == 1)
+    def _():
+        for share in (across[2], across[1], across[3], across[0]):
+            share.start()
+
     for share in shares:
         share.start()
 
     @pl.when(flank == 0)
     def _():
         pl.semaphore_wait(met, n_proj)
-
-    across = [pass_on(k, t_send.at[peer(k)], t_mate, us_sem, ur_sem) for k in range(n_proj)]
-    for share in across:
-        share.start()
+        for share in across:
+            share.start()
 
     l_at = lax.broadcasted_iota(jnp.int32, (128, kc), 0)
     k_at = lax.broadcasted_iota(jnp.int32, (128, kc), 1)
@@ -491,28 +495,40 @@
             device_id=(grp, me_ex, me), device_id_type=MESH,
         )
 
-    block = rows[:, pl.ds(pl.multiple_of(me * kc, 128), kc)]
-    for k, share in enumerate(shares):
-        share.wait_recv()
-        block = block + t_in[k].astype(F32)
-    train = score(0, block)
-    for jj in range(per):
-        @pl.when(me != flank * per + jj)
-        def _():
-            report(0, jj).start()
-
-        @pl.when(me == flank * per + jj)
-        def _():
-            f_recv[me] = f_send[0, jj]
-    block = jnp.zeros((ex_dev * pd, kc), F32)
-    for k, share in enumerate(across):
-        share.wait_recv()
-        block = block + t_mate[k].astype(F32)
-    score(1, block)
-    for jj in range(per):
-        report(1, jj).start()
-
-    tp_ref[...] = train
+    def own_stage():
+        block = rows[:, pl.ds(pl.multiple_of(me * kc, 128), kc)]
+        for k, share in enumerate(shares):
+            share.wait_recv()
+            block = block + t_in[k].astype(F32)
+        tp_ref[...] = score(0, block)
+        for jj in range(per):
+            @pl.when(me != flank * per + jj)
+            def _():
+                report(0, jj).start()
+
+            @pl.when(me == flank * per + jj)
+            def _():
+                f_recv[me] = f_send[0, jj]
+
+    def mate_stage():
+        block = jnp.zeros((ex_dev * pd, kc), F32)
+        for k, share in enumerate(across):
+            share.wait_recv()
+            block = block + t_mate[k].astype(F32)
+        score(1, block)
+        for jj in range(per):
+            report(1, jj).start()
+
+    @pl.when(flank == 0)
+    def _():
+        own_stage()
+        mate_stage()
+
+    @pl.when(flank == 1)
+    def _():
+        mate_stage()
+        own_stage()
+
     for move in moves + shares + across:
         move.wait_send()
     for i in range(n_ex):

time: 16.6 us -> 16.3 us (0.982)
  the two profiles are of different devices: /device:TPU:25 before, /device:TPU:0 now
where the time goes in v4:
time: 16.3 us; the launch traced here: 16.1 us
  Pallas kernels  15.5 us (95%)
  between operations  0.64 us (4%)
    pallas_call x1, Pallas kernels, shards(): pl.pallas_call(functools.partial(body, (n_ex, n_proj, ex_dev, seq, pdim))...  14.8 us
    pallas_call x1, Pallas kernels, shards(): pl.pallas_call(functools.partial(end, pdim), out_shape=(jax.ShapeDtypeStr...  0.66 us

profile of v4, /device:TPU:0, one launch (start us, length us, event | category | flops | bytes accessed | tf_op | source)
XLA Modules:
  0.0 16.1 jit_solution(5904812618136477529)
XLA Ops:
  0.6 14.8 %project.1 = (f32[8,2048]{1,0:T(8,128)S(1)}, f32[8,128]{1,0:T(8,128)S(1)}) custom-call(s32[4]{0:T(128)} %len_hbm.1, bf16[576,1280]{1,0:T(8,128)(2,1)} %bitcast.3, bf16[576,1280]{1,0:T(8,128)(2,1)} %bitcast.4, bf16[128,1280]{1,0:T(8,128)(2,1)} %a_ref.1, bf16[1280,128]{1,0:T(8,128)(2,1)} %b_ref.1, bf16[1280,512]{1,0:T(8,128)(2,1)} %w_ref.1, ...), custom_call_target="tpu_custom_call" | custom-call | tf_op jit(solution)/shard_map/project/pallas_call | solution.py:667
  15.4 0.7 %finish.1 = (bf16[4,2048]{1,0:T(4,128)(2,1)}, f32[4,32]{1,0:T(4,128)}) custom-call(f32[8,2048]{1,0:T(8,128)S(1)} %get-tuple-element.4.train_ref, f32[8,128]{1,0:T(8,128)S(1)} %get-tuple-element.5.sums_ref), custom_call_target="tpu_custom_call" | custom-call | tf_op jit(solution)/shard_map/finish/pallas_call | solution.py:685

commit v5 on v4

--- a/solution.py
+++ b/solution.py
@@ -261,8 +261,8 @@
     sizes,
     len_hbm, x_ref, c_ref, a_ref, b_ref, w_ref, r_hbm, v_ref,
     tp_ref, sc_ref,
-    xb, cb, ab, bb, wb, r_ref, len_ref, held, rows, right_own, right_in, t_send, t_in, t_mate, shuf, flat, f_send, f_recv,
-    load_sem, rs_sem, rr_sem, ts_sem, tr_sem, us_sem, ur_sem, hs_sem, hr_sem, fs_sem, fr_sem, own_sem, ready, met,
+    xb, cb, ab, bb, wb, r_ref, len_ref, held, left, rows, right_own, right_in, t_send, t_in, t_mate, shuf, flat, f_send, f_recv,
+    load_sem, rs_sem, rr_sem, ts_sem, tr_sem, us_sem, ur_sem, hs_sem, hr_sem, fs_sem, fr_sem, own_sem, ready, met, near,
 ):
     n_ex, n_proj, ex_dev, seq, pdim = sizes
     grp, me_ex, me = lax.axis_index("grp"), lax.axis_index("ex"), lax.axis_index("proj")
@@ -294,8 +294,10 @@
         copy = pltpu.make_async_copy(src, dst, load_sem.at[i])
         copy.start()
         loads.append(copy)
-    for k in range(1, n_proj):
-        greet(me_ex, peer(k))
+    for q in range(1, n_proj):
+        @pl.when(q > me)
+        def _():
+            greet(me_ex, q)
     for i in range(1, n_ex):
         @pl.when(i > me_ex)
         def _():
@@ -305,7 +307,7 @@
     def _():
         for k in range(1, n_proj):
             greet(mate, peer(k))
-    expected = n_proj - 1 + me_ex + flank * (n_proj - 1)
+    expected = me + me_ex + flank * (n_proj - 1)
 
     def place(jj):
         return held.at[pl.ds(jj * v_rows, v_rows)]
@@ -340,47 +342,41 @@
             device_id=(grp, me_ex, peer(k)), device_id_type=MESH,
         )
 
+    @pl.when(expected > 0)
+    def _():
+        pl.semaphore_wait(barrier, expected)
+
+    for j in range(n_ex - 1):
+        @pl.when((j < me_ex) & (j // per == flank))
+        def _():
+            pl.semaphore_signal(
+                ready.at[me_ex], inc=1, device_id=(grp, j, me), device_id_type=MESH
+            )
+
+    for i in range(n_ex - 1):
+        @pl.when((i < me_ex) & (i % 2 == home))
+        def _():
+            give(i).start()
+
+    @pl.when(flank == 1)
+    def _():
+        for k in range(n_proj):
+            pl.semaphore_signal(
+                met, inc=1, device_id=(grp, mate, peer(k)), device_id_type=MESH
+            )
+
+    for q in range(n_proj - 1):
+        @pl.when(q < me)
+        def _():
+            pl.semaphore_signal(near, inc=1, device_id=(grp, me_ex, q), device_id_type=MESH)
+
     flat[...] = jnp.zeros_like(flat)
     for copy in loads[:3]:
         copy.wait()
     m_in = dot(r_ref[0], ab[...]).astype(BF16)
     m_out = dot(r_ref[1], bb[...], NT).astype(BF16)
-    @pl.when(me_ex > 0)
-    def _():
-        pl.semaphore_wait(barrier, expected)
-        for j in range(n_ex - 1):
-            @pl.when((j < me_ex) & (j // per == flank))
-            def _():
-                pl.semaphore_signal(
-                    ready.at[me_ex], inc=1, device_id=(grp, j, me), device_id_type=MESH
-                )
-
-        for i in range(n_ex - 1):
-            @pl.when((i < me_ex) & (i % 2 == home))
-            def _():
-                give(i).start()
-
-        @pl.when(flank == 1)
-        def _():
-            for k in range(n_proj):
-                pl.semaphore_signal(
-                    met, inc=1, device_id=(grp, mate, peer(k)), device_id_type=MESH
-                )
-
     loads[3].wait()
     part_in = dot(m_in, xb[...], NT)
-    loads[4].wait()
-    part_out = dot(m_out, cb[...], NT)
-    part = jnp.concatenate([part_in, part_out], axis=0)
-    right_own[...] = part.astype(BF16)
-
-    @pl.when(me_ex == 0)
-    def _():
-        pl.semaphore_wait(barrier, expected)
-
-    moves = [swap(k, right_own, right_in, rs_sem, rr_sem) for k in range(1, n_proj)]
-    for move in moves:
-        move.start()
     def give_later(k):
         for i in range(k, n_ex):
             @pl.when((i == me_ex + k) & (i % 2 == home))
@@ -388,8 +384,31 @@
                 pl.semaphore_wait(ready.at[i], 1)
                 give(i).start()
 
-    for k in range(1, n_ex):
+    @pl.when(flank == 1)
+    def _():
+        give_later(1)
+
+    loads[4].wait()
+    part_out = dot(m_out, cb[...], NT)
+    part = jnp.concatenate([part_in, part_out], axis=0)
+    right_own[...] = part.astype(BF16)
+
+    @pl.when(me < n_proj - 1)
+    def _():
+        pl.semaphore_wait(near, n_proj - 1 - me)
+
+    moves = [swap(k, right_own, right_in, rs_sem, rr_sem) for k in range(1, n_proj)]
+    for move in moves:
+        move.start()
+    @pl.when(flank == 0)
+    def _():
+        give_later(1)
+
+    for k in range(2, n_ex):
         give_later(k)
+    loads[5].wait()
+    left[0] = dot(cb[...], wb[...]).astype(BF16)
+    left[1] = dot(xb[...], wb[...]).astype(BF16)
 
     loads[6].wait()
     position = lax.broadcasted_iota(jnp.int32, (k2, tokens), 1)
@@ -405,13 +424,12 @@
         move.wait_recv()
         total = total + right_in[k].astype(F32)
     total = total.astype(BF16).astype(F32)
-    grown = []
-    for p, other in enumerate((cb, xb)):
+    result = []
+    for p in range(2):
         piece = total[p * k2:(p + 1) * k2]
         spread = jnp.concatenate([jnp.where(one, piece, 0.0) for one in live], axis=0).astype(BF16)
-        grown.append(dot(spread, other[...]))
-    loads[5].wait()
-    result = dot(jnp.concatenate(grown, axis=0).astype(BF16), wb[...])
+        result.append(dot(spread, left[p]))
+    result = jnp.concatenate(result, axis=0)
     for p in range(2):
         for e in range(ex_dev):
             at = (p * ex_dev + e) * k2
@@ -619,6 +637,7 @@
             pltpu.VMEM((2, k2, rank), BF16),
             pltpu.SMEM((ex_dev,), jnp.int32),
             pltpu.VMEM((per * v_rows, v_cols), BF16),
+            pltpu.VMEM((2, tokens, k1), BF16),
             pltpu.VMEM((ex_dev * pd, k1), F32),
             pltpu.VMEM((pd, tokens), BF16),
             pltpu.VMEM((peers, pd, tokens), BF16),
@@ -637,6 +656,7 @@
             dma((2, per)), dma((n_proj,)),
             dma,
             pltpu.SemaphoreType.REGULAR((n_ex,)),
+            pltpu.SemaphoreType.REGULAR,
             pltpu.SemaphoreType.REGULAR,
         ]
     else:

time: 16.3 us -> 15.7 us (0.963)
  the two profiles are of different devices: /device:TPU:0 before, /device:TPU:25 now
where the time goes in v5:
time: 15.7 us; the launch traced here: 15.4 us
  Pallas kernels  14.8 us (94%)
  between operations  0.64 us (4%)
    pallas_call x1, Pallas kernels, shards(): pl.pallas_call(functools.partial(body, (n_ex, n_proj, ex_dev, seq, pdim))...  14.1 us
    pallas_call x1, Pallas kernels, shards(): pl.pallas_call(functools.partial(end, pdim), out_shape=(jax.ShapeDtypeStr...  0.66 us

profile of v5, /device:TPU:25, one launch (start us, length us, event | category | flops | bytes accessed | tf_op | source)
XLA Modules:
  0.0 15.4 jit_solution(15872583682478988697)
XLA Ops:
  0.6 14.1 %project.1 = (f32[8,2048]{1,0:T(8,128)S(1)}, f32[8,128]{1,0:T(8,128)S(1)}) custom-call(s32[4]{0:T(128)} %len_hbm.1, bf16[576,1280]{1,0:T(8,128)(2,1)} %bitcast.3, bf16[576,1280]{1,0:T(8,128)(2,1)} %bitcast.4, bf16[128,1280]{1,0:T(8,128)(2,1)} %a_ref.1, bf16[1280,128]{1,0:T(8,128)(2,1)} %b_ref.1, bf16[1280,512]{1,0:T(8,128)(2,1)} %w_ref.1, ...), custom_call_target="tpu_custom_call" | custom-call | tf_op jit(solution)/shard_map/project/pallas_call | solution.py:687
  14.8 0.7 %finish.1 = (bf16[4,2048]{1,0:T(4,128)(2,1)}, f32[4,32]{1,0:T(4,128)}) custom-call(f32[8,2048]{1,0:T(8,128)S(1)} %get-tuple-element.4.train_ref, f32[8,128]{1,0:T(8,128)S(1)} %get-tuple-element.5.sums_ref), custom_call_target="tpu_custom_call" | custom-call | tf_op jit(solution)/shard_map/finish/pallas_call | solution.py:705

commit v6 on v5

--- a/solution.py
+++ b/solution.py
@@ -377,6 +377,21 @@
     m_out = dot(r_ref[1], bb[...], NT).astype(BF16)
     loads[3].wait()
     part_in = dot(m_in, xb[...], NT)
+    right_own[0] = part_in.astype(BF16)
+
+    @pl.when(me < n_proj - 1)
+    def _():
+        pl.semaphore_wait(near, n_proj - 1 - me)
+
+    def share_right(p):
+        started = [
+            swap(k, right_own.at[p], right_in.at[p], rs_sem.at[p], rr_sem.at[p]) for k in range(1, n_proj)
+        ]
+        for move in started:
+            move.start()
+        return started
+
+    moves = [share_right(0)]
     def give_later(k):
         for i in range(k, n_ex):
             @pl.when((i == me_ex + k) & (i % 2 == home))
@@ -390,16 +405,9 @@
 
     loads[4].wait()
     part_out = dot(m_out, cb[...], NT)
-    part = jnp.concatenate([part_in, part_out], axis=0)
-    right_own[...] = part.astype(BF16)
-
-    @pl.when(me < n_proj - 1)
-    def _():
-        pl.semaphore_wait(near, n_proj - 1 - me)
-
-    moves = [swap(k, right_own, right_in, rs_sem, rr_sem) for k in range(1, n_proj)]
-    for move in moves:
-        move.start()
+    right_own[1] = part_out.astype(BF16)
+    moves.append(share_right(1))
+
     @pl.when(flank == 0)
     def _():
         give_later(1)
@@ -419,14 +427,12 @@
         live.append((position >= e * seq) & (position < e * seq + count))
         scale.append(1.0 / jnp.full((k2, 128), count.astype(F32), F32))
 
-    total = part
-    for k, move in enumerate(moves):
-        move.wait_recv()
-        total = total + right_in[k].astype(F32)
-    total = total.astype(BF16).astype(F32)
     result = []
-    for p in range(2):
-        piece = total[p * k2:(p + 1) * k2]
+    for p, piece in enumerate((part_in, part_out)):
+        for k, move in enumerate(moves[p]):
+            move.wait_recv()
+            piece = piece + right_in[p, k].astype(F32)
+        piece = piece.astype(BF16).astype(F32)
         spread = jnp.concatenate([jnp.where(one, piece, 0.0) for one in live], axis=0).astype(BF16)
         result.append(dot(spread, left[p]))
     result = jnp.concatenate(result, axis=0)
@@ -547,7 +553,7 @@
         mate_stage()
         own_stage()
 
-    for move in moves + shares + across:
+    for move in moves[0] + moves[1] + shares + across:
         move.wait_send()
     for i in range(n_ex):
         @pl.when((i != me_ex) & (i % 2 == home))
@@ -639,8 +645,8 @@
             pltpu.VMEM((per * v_rows, v_cols), BF16),
             pltpu.VMEM((2, tokens, k1), BF16),
             pltpu.VMEM((ex_dev * pd, k1), F32),
-            pltpu.VMEM((pd, tokens), BF16),
-            pltpu.VMEM((peers, pd, tokens), BF16),
+            pltpu.VMEM((2, k2, tokens), BF16),
+            pltpu.VMEM((2, peers, k2, tokens), BF16),
             pltpu.VMEM((n_proj, ex_dev * pd, kc), BF16),
             pltpu.VMEM((peers, ex_dev * pd, kc), BF16),
             pltpu.VMEM((n_proj, ex_dev * pd, kc), BF16),
@@ -649,7 +655,7 @@
             pltpu.VMEM((2, per, ep, 128), F32),
             pltpu.VMEM((n_proj, ep, 128), F32),
             dma((7,)),
-            dma((peers,)), dma((peers,)),
+            dma((2, peers)), dma((2, peers)),
             dma((peers,)), dma((peers,)),
             dma((n_proj,)), dma((n_proj,)),
             dma((n_ex,)), dma((per,)),

time: 15.7 us -> 15.7 us (level)
  no operation moved by 1% of the time
where the time goes in v6:
time: 15.7 us; the launch traced here: 15.5 us
  Pallas kernels  14.8 us (94%)
  between operations  0.64 us (4%)
    pallas_call x1, Pallas kernels, shards(): pl.pallas_call(functools.partial(body, (n_ex, n_proj, ex_dev, seq, pdim))...  14.2 us
    pallas_call x1, Pallas kernels, shards(): pl.pallas_call(functools.partial(end, pdim), out_shape=(jax.ShapeDtypeStr...  0.66 us

profile of v6, /device:TPU:25, one launch (start us, length us, event | category | flops | bytes accessed | tf_op | source)
XLA Modules:
  0.0 15.5 jit_solution(9468369729427849608)
XLA Ops:
  0.6 14.2 %project.1 = (f32[8,2048]{1,0:T(8,128)S(1)}, f32[8,128]{1,0:T(8,128)S(1)}) custom-call(s32[4]{0:T(128)} %len_hbm.1, bf16[576,1280]{1,0:T(8,128)(2,1)} %bitcast.3, bf16[576,1280]{1,0:T(8,128)(2,1)} %bitcast.4, bf16[128,1280]{1,0:T(8,128)(2,1)} %a_ref.1, bf16[1280,128]{1,0:T(8,128)(2,1)} %b_ref.1, bf16[1280,512]{1,0:T(8,128)(2,1)} %w_ref.1, ...), custom_call_target="tpu_custom_call" | custom-call | tf_op jit(solution)/shard_map/project/pallas_call | solution.py:693
  14.8 0.7 %finish.1 = (bf16[4,2048]{1,0:T(4,128)(2,1)}, f32[4,32]{1,0:T(4,128)}) custom-call(f32[8,2048]{1,0:T(8,128)S(1)} %get-tuple-element.4.train_ref, f32[8,128]{1,0:T(8,128)S(1)} %get-tuple-element.5.sums_ref), custom_call_target="tpu_custom_call" | custom-call | tf_op jit(solution)/shard_map/finish/pallas_call | solution.py:711

commit v7 on v6

--- a/solution.py
+++ b/solution.py
@@ -524,7 +524,7 @@
         for k, share in enumerate(shares):
             share.wait_recv()
             block = block + t_in[k].astype(F32)
-        tp_ref[...] = score(0, block)
+        train = score(0, block)
         for jj in range(per):
             @pl.when(me != flank * per + jj)
             def _():
@@ -533,6 +533,7 @@
             @pl.when(me == flank * per + jj)
             def _():
                 f_recv[me] = f_send[0, jj]
+        tp_ref[...] = train
 
     def mate_stage():
         block = jnp.zeros((ex_dev * pd, kc), F32)

time: 15.7 us -> 15.7 us (level)
  no operation moved by 1% of the time
where the time goes in v7:
time: 15.7 us; the launch traced here: 15.5 us
  Pallas kernels  14.8 us (94%)
  between operations  0.64 us (4%)
    pallas_call x1, Pallas kernels, shards(): pl.pallas_call(functools.partial(body, (n_ex, n_proj, ex_dev, seq, pdim))...  14.2 us
    pallas_call x1, Pallas kernels, shards(): pl.pallas_call(functools.partial(end, pdim), out_shape=(jax.ShapeDtypeStr...  0.66 us

profile of v7, /device:TPU:25, one launch (start us, length us, event | category | flops | bytes accessed | tf_op | source)
XLA Modules:
  0.0 15.5 jit_solution(12561335574711454048)
XLA Ops:
  0.6 14.2 %project.1 = (f32[8,2048]{1,0:T(8,128)S(1)}, f32[8,128]{1,0:T(8,128)S(1)}) custom-call(s32[4]{0:T(128)} %len_hbm.1, bf16[576,1280]{1,0:T(8,128)(2,1)} %bitcast.3, bf16[576,1280]{1,0:T(8,128)(2,1)} %bitcast.4, bf16[128,1280]{1,0:T(8,128)(2,1)} %a_ref.1, bf16[1280,128]{1,0:T(8,128)(2,1)} %b_ref.1, bf16[1280,512]{1,0:T(8,128)(2,1)} %w_ref.1, ...), custom_call_target="tpu_custom_call" | custom-call | tf_op jit(solution)/shard_map/project/pallas_call | solution.py:694
  14.8 0.7 %finish.1 = (bf16[4,2048]{1,0:T(4,128)(2,1)}, f32[4,32]{1,0:T(4,128)}) custom-call(f32[8,2048]{1,0:T(8,128)S(1)} %get-tuple-element.4.train_ref, f32[8,128]{1,0:T(8,128)S(1)} %get-tuple-element.5.sums_ref), custom_call_target="tpu_custom_call" | custom-call | tf_op jit(solution)/shard_map/finish/pallas_call | solution.py:712
